TPU v7x, 32 devices: a whole 2x2x4 slice. The times are simulated.
32 devices in a mesh: ctx: 8 (over y, x, core), head: 4 (over z).
Axes of the slice: x: 2, y: 2, z: 4, core: 2. Of those that a mesh axis runs over, the one named last changes fastest.
Arguments:
- routed_q: bfloat16 [4096, 1024], P('ctx', 'head'), may hold values from -16 to 16
- routed_k: bfloat16 [4096, 1024], P('ctx', 'head'), may hold values from -16 to 16
- routed_v: bfloat16 [4096, 1024], P('ctx', 'head'), may hold values from -6 to 6
- routed_grad: bfloat16 [4096, 1024], P('ctx', 'head'), may hold values from -6 to 6
- local_q: bfloat16 [4096, 1024], P('ctx', 'head'), may hold values from -16 to 16
- local_k: bfloat16 [4096, 1024], P('ctx', 'head'), may hold values from -16 to 16
- local_v: bfloat16 [4096, 1024], P('ctx', 'head'), may hold values from -6 to 6
- local_grad: bfloat16 [4096, 1024], P('ctx', 'head'), may hold values from -6 to 6
- clusters: int32 [8, 4096], P('head', 'ctx'), may hold values from 0 to 63, as said below
- cluster_slot: int32 [8, 64], P('head'), may hold values from 0 to 63, each once within a row
- rel_bias: float32 [128], replicated, may hold values from -4 to 4
Outputs:
- routed_out: bfloat16 [4096, 1024], P('ctx', 'head')
- routed_dq: bfloat16 [4096, 1024], P('ctx', 'head')
- routed_dk: bfloat16 [4096, 1024], P('ctx', 'head')
- routed_dv: bfloat16 [4096, 1024], P('ctx', 'head')
- centroids: float32 [8, 64, 128], P('head', 'ctx')
- local_out: bfloat16 [4096, 1024], P('ctx', 'head')
- local_dq: bfloat16 [4096, 1024], P('ctx', 'head')
- local_dk: bfloat16 [4096, 1024], P('ctx', 'head')
- local_dv: bfloat16 [4096, 1024], P('ctx', 'head')
- bias_grad: float32 [128], replicated
Inputs may be any that keep to these rules, and one draw needn't show every extreme that they name: `clusters`: among the 512 positions of one index of ctx, at most 16 name the same cluster for one routed head; for every routed head one cluster is named exactly 16 times on every index of ctx.
All inputs are finite; a program needn't handle non-finite values.
Results may differ from a plain program's by a relative error of at most 0.0077.
Values may be sent and summed in bfloat16 or wider, within the bound.
No kernel may reach another device: no remote copies, remote signals or barrier semaphores. Data moves between devices by JAX's collectives and lax.ppermute only.
A program may use at most 64 MiB of HBM per device.

v0:
```python
import jax
import jax.numpy as jnp
from jax import lax
from jax.experimental import pallas as pl
from jax.experimental.pallas import tpu as pltpu
from jax.sharding import PartitionSpec as P


HEAD_DIM = 128
WINDOW = 128

NEG = -1e30
EPSILON = 1e-06
EMPTY = 64.0
EMPTY_LEVEL = 32.0

PARAMS = pltpu.CompilerParams(vmem_limit_bytes=16 << 20)

F32 = jnp.float32
BF16 = jnp.bfloat16


def dot_nn(a, b):
    return lax.dot_general(a, b, (((1,), (0,)), ((), ())), preferred_element_type=F32)


def dot_nt(a, b):
    return lax.dot_general(a, b, (((1,), (1,)), ((), ())), preferred_element_type=F32)


def dot_tn(a, b):
    return lax.dot_general(a, b, (((0,), (0,)), ((), ())), preferred_element_type=F32)


def iota(shape, dim):
    return lax.broadcasted_iota(jnp.int32, shape, dim)


def softmax_down(scores, dprobs):
    exponent = jnp.exp(scores - jnp.max(scores, axis=0, keepdims=True))
    probs = exponent * (1.0 / jnp.sum(exponent, axis=0, keepdims=True))
    weighted = probs * dprobs
    return probs, weighted - probs * jnp.sum(weighted, axis=0, keepdims=True)


def pack_kernel(me_ref, ids_ref, slots_ref, q_ref, k_ref, v_ref, g_ref, flat_ref, *out_refs, head, per_source):
    ids = ids_ref[head : head + 1, :]
    tokens = ids.shape[1]
    clusters = slots_ref.shape[1]
    rows = out_refs[0].shape[0]
    member = iota((clusters, tokens), 0) == ids
    member_low = jnp.where(member, 1.0, 0.0).astype(BF16)
    earlier = jnp.where(iota((tokens, tokens), 0) < iota((tokens, tokens), 1), 1.0, 0.0).astype(BF16)
    before = dot_nn(member_low, earlier)
    rank = jnp.sum(jnp.where(member, before, 0.0), axis=0, keepdims=True)
    slots = jnp.broadcast_to(slots_ref[head : head + 1, :], (8, clusters)).astype(F32).astype(BF16)
    flat = dot_nn(slots, member_low)[:1] * per_source + rank
    flat_ref[...] = jnp.broadcast_to(flat, flat_ref.shape)
    where_to = flat.astype(jnp.int32)
    data = jnp.concatenate([q_ref[...], k_ref[...], v_ref[...], g_ref[...]], axis=1)
    dim = k_ref.shape[1]
    me = me_ref[0, 0]
    slot = iota((rows, tokens), 0)
    chosen = [jnp.where(slot == where_to - (me ^ m) * rows, 1.0, 0.0) for m in range(len(out_refs))]
    moved = dot_nn(jnp.concatenate([c.astype(BF16) for c in chosen], axis=0), data)
    first_col = iota((rows, dim), 1) == 0
    for m, out_ref in enumerate(out_refs):
        part = moved[m * rows : (m + 1) * rows]
        filled = jnp.sum(chosen[m], axis=1, keepdims=True) > 0.5
        marked = jnp.where(first_col & ~filled, EMPTY, part[:, dim : 2 * dim])
        out_ref[:, :dim] = part[:, :dim].astype(BF16)
        out_ref[:, dim : 2 * dim] = marked.astype(BF16)
        out_ref[:, 2 * dim :] = part[:, 2 * dim :].astype(BF16)


def scalar_spec():
    return pl.BlockSpec((1, 1), lambda *_: (0, 0), memory_space=pltpu.SMEM)


def whole(array):
    return pl.BlockSpec(array.shape, lambda *_: (0,) * array.ndim)


def pack(me, ids, slots, arrays, head, dests, per_source):
    tokens = arrays[0].shape[0]
    clusters = slots.shape[1]
    rows = clusters * per_source // dests
    width = len(arrays) * HEAD_DIM
    column = pl.BlockSpec((tokens, HEAD_DIM), lambda i: (0, head))
    shapes = [jax.ShapeDtypeStruct((8, tokens), F32)]
    shapes += [jax.ShapeDtypeStruct((rows, width), BF16)] * dests
    flat, *chunks = pl.pallas_call(
        lambda *refs: pack_kernel(*refs, head=head, per_source=per_source),
        grid=(1,),
        in_specs=[scalar_spec(), whole(ids), whole(slots)] + [column] * 4,
        out_specs=[whole(s) for s in shapes],
        out_shape=shapes,
        name="pack",
        compiler_params=PARAMS,
    )(me, ids, slots, *arrays)
    return flat, chunks


def owner_kernel(me_ref, *refs, per_source, sources):
    got_refs = refs[:sources]
    out_refs = refs[-sources - 1 : -1]
    centroid_ref = refs[-1]
    dim = HEAD_DIM
    capacity = sources * per_source
    clusters = got_refs[0].shape[0] // per_source
    key = iota((capacity, capacity), 0)
    query = iota((capacity, capacity), 1)
    base = me_ref[0, 0] * per_source
    causal = (key ^ base) <= (query ^ base)
    diagonal = key == query
    first_col = iota((capacity, dim), 1) == 0
    scaling = dim ** (-0.5)
    spots = [slice(c * per_source, (c + 1) * per_source) for c in range(clusters)]

    def gathered(part):
        at = slice(part * dim, (part + 1) * dim)
        return [jnp.concatenate([ref[spot, at] for ref in got_refs], axis=0) for spot in spots]

    def scatter(part, results):
        at = slice(part * dim, (part + 1) * dim)
        for spot, result in zip(spots, results):
            for m, ref in enumerate(out_refs):
                ref[spot, at] = result[m * per_source : (m + 1) * per_source].astype(BF16)

    queries, keys, values, cots = (gathered(part) for part in range(4))
    scores, sums = [], []
    for q, k in zip(queries, keys):
        wide = k.astype(F32)
        live = wide[:, :1] < EMPTY_LEVEL
        scores.append(jnp.where((live & causal) | diagonal, dot_nt(k, q) * scaling, NEG))
        sums.append(jnp.sum(jnp.where(first_col & ~live, 0.0, wide), axis=0, keepdims=True))
    dprobs = [dot_nt(v, g) for v, g in zip(values, cots)]
    both = [softmax_down(s, d) for s, d in zip(scores, dprobs)]
    probs = [p.astype(BF16) for p, _ in both]
    dscores = [d.astype(BF16) for _, d in both]
    scatter(0, [dot_tn(p, v) for p, v in zip(probs, values)])
    scatter(3, [dot_nn(p, g) for p, g in zip(probs, cots)])
    scatter(2, [dot_nn(d, q) * scaling for d, q in zip(dscores, queries)])
    scatter(1, [dot_tn(d, k) * scaling for d, k in zip(dscores, keys)])
    key_sums = jnp.concatenate(sums, axis=0)
    norm = jnp.sqrt(jnp.mean(key_sums * key_sums, axis=-1, keepdims=True) + EPSILON)
    centroid_ref[0] = key_sums / norm


def owner(me, got, per_source, head, heads, previous):
    rows, width = got[0].shape
    shapes = [jax.ShapeDtypeStruct((rows, width), BF16)] * len(got)
    held = jax.ShapeDtypeStruct((heads, rows // per_source, HEAD_DIM), F32)
    any_spec = pl.BlockSpec(memory_space=pl.ANY)
    *back, centroids = pl.pallas_call(
        lambda *refs: owner_kernel(*refs, per_source=per_source, sources=len(got)),
        grid=(1,),
        in_specs=[scalar_spec()] + [whole(g) for g in got] + [any_spec] * len(previous),
        out_specs=[whole(s) for s in shapes]
        + [pl.BlockSpec((1,) + held.shape[1:], lambda i: (head, 0, 0))],
        out_shape=shapes + [held],
        input_output_aliases={1 + len(got) + n: len(got) + n for n in range(len(previous))},
        name="owner",
        compiler_params=PARAMS,
    )(me, *got, *previous)
    return back, centroids


def unpack_kernel(me_ref, flat_ref, *refs, chunks):
    home_refs = refs[:chunks]
    width = home_refs[0].shape[1]
    out_refs = refs[-(width // HEAD_DIM) :]
    tokens = flat_ref.shape[1]
    rows = home_refs[0].shape[0]
    wide = jnp.broadcast_to(flat_ref[:1, :], (HEAD_DIM, tokens)).T.astype(jnp.int32)[:, :rows]
    lane = iota((tokens, rows), 1)
    chosen = jnp.concatenate(
        [
            jnp.where(wide - (me_ref[0, 0] ^ m) * rows == lane, 1.0, 0.0).astype(BF16)
            for m in range(chunks)
        ],
        axis=1,
    )
    home = jnp.concatenate([ref[...] for ref in home_refs], axis=0)
    moved = dot_nn(chosen, home).astype(BF16)
    for n, out_ref in enumerate(out_refs):
        out_ref[...] = moved[:, n * HEAD_DIM : (n + 1) * HEAD_DIM]


def unpack(me, flat, home, head, heads, previous):
    tokens = flat.shape[1]
    outs = home[0].shape[1] // HEAD_DIM
    any_spec = pl.BlockSpec(memory_space=pl.ANY)
    return pl.pallas_call(
        lambda *refs: unpack_kernel(*refs, chunks=len(home)),
        grid=(1,),
        in_specs=[scalar_spec(), whole(flat)] + [whole(h) for h in home] + [any_spec] * len(previous),
        out_specs=[pl.BlockSpec((tokens, HEAD_DIM), lambda i: (0, head))] * outs,
        out_shape=[jax.ShapeDtypeStruct((tokens, heads * HEAD_DIM), BF16)] * outs,
        input_output_aliases={2 + len(home) + n: n for n in range(len(previous))},
        name="unpack",
        compiler_params=PARAMS,
    )(me, flat, *home, *previous)


def exchange(chunks):
    size = len(chunks)
    moved = [chunks[0]] + [None] * (size - 1)
    for m in reversed(range(1, size)):
        moved[m] = lax.ppermute(chunks[m], "ctx", [(i, i ^ m) for i in range(size)])
    return moved


def shift_rows(array, sign):
    count, lanes = array.shape
    row = iota((count, lanes), 0)
    step = 1
    while step < count:
        rolled = pltpu.roll(array, step if sign > 0 else lanes - step, 1)
        array = jnp.where((row & step) != 0, rolled, array)
        step *= 2
    return array


def halo_kernel(hq_ref, hk_ref, hv_ref, hg_ref, tk_ref, tv_ref, lead_ref, tail_ref):
    width = hq_ref.shape[1]
    for n, ref in enumerate((hq_ref, hk_ref, hv_ref, hg_ref)):
        lead_ref[:, n * width : (n + 1) * width] = ref[...]
    for n, ref in enumerate((tk_ref, tv_ref)):
        tail_ref[:, n * width : (n + 1) * width] = ref[...]


def halo_pieces(own):
    tokens, width = own[0].shape
    head = pl.BlockSpec((WINDOW, width), lambda i: (0, 0))
    last = pl.BlockSpec((WINDOW, width), lambda i: (tokens // WINDOW - 1, 0))
    shapes = [jax.ShapeDtypeStruct((WINDOW, n * width), BF16) for n in (4, 2)]
    return pl.pallas_call(
        halo_kernel,
        grid=(1,),
        in_specs=[head] * 4 + [last] * 2,
        out_specs=[whole(s) for s in shapes],
        out_shape=shapes,
        name="halo",
        compiler_params=PARAMS,
    )(*own, own[1], own[2])


def local_kernel(
    first_ref,
    bias_ref,
    q_ref,
    k_ref,
    v_ref,
    g_ref,
    pk_ref,
    pv_ref,
    nq_ref,
    nk_ref,
    nv_ref,
    ng_ref,
    out_ref,
    dq_ref,
    dk_ref,
    dv_ref,
    part_ref,
):
    tokens, dim = q_ref.shape
    scaling = dim ** (-0.5)
    count = tokens // WINDOW
    size = (WINDOW, WINDOW)
    early = iota(size, 1) < iota(size, 0)
    bias = shift_rows(jnp.broadcast_to(bias_ref[...], size), 1)
    bias_first = jnp.where(early & (first_ref[0, 0] > 0), NEG, bias)
    spots = [slice(b * WINDOW, (b + 1) * WINDOW) for b in range(count)]
    queries = [q_ref[s] for s in spots] + [nq_ref[...]]
    cots = [g_ref[s] for s in spots] + [ng_ref[...]]
    keys = [pk_ref[...]] + [k_ref[s] for s in spots] + [nk_ref[...]]
    values = [pv_ref[...]] + [v_ref[s] for s in spots] + [nv_ref[...]]
    scores = [
        jnp.where(early, dot_nt(keys[b], queries[b]), dot_nt(keys[b + 1], queries[b])) * scaling
        + (bias if b else bias_first)
        for b in range(count + 1)
    ]
    dprobs = [
        jnp.where(early, dot_nt(values[b], cots[b]), dot_nt(values[b + 1], cots[b]))
        for b in range(count + 1)
    ]
    both = [softmax_down(s, d) for s, d in zip(scores, dprobs)]
    total = both[0][1]
    for b in range(1, count):
        total = total + both[b][1]
    zero = jnp.zeros(size, F32)
    probs = [
        (jnp.where(early, p, zero).astype(BF16), jnp.where(early, zero, p).astype(BF16)) for p, _ in both
    ]
    dscores = [
        (jnp.where(early, d, zero).astype(BF16), jnp.where(early, zero, d).astype(BF16)) for _, d in both
    ]
    for b, s in enumerate(spots):
        out_ref[s] = (dot_tn(probs[b][0], values[b]) + dot_tn(probs[b][1], values[b + 1])).astype(BF16)
        dv_ref[s] = (dot_nn(probs[b][1], cots[b]) + dot_nn(probs[b + 1][0], cots[b + 1])).astype(BF16)
        dk = dot_nn(dscores[b][1], queries[b]) + dot_nn(dscores[b + 1][0], queries[b + 1])
        dk_ref[s] = (dk * scaling).astype(BF16)
        dq = dot_tn(dscores[b][0], keys[b]) + dot_tn(dscores[b][1], keys[b + 1])
        dq_ref[s] = (dq * scaling).astype(BF16)
    part = jnp.sum(shift_rows(total, -1), axis=0, keepdims=True)
    part = jnp.broadcast_to(part[None], part_ref.shape)

    @pl.when(pl.program_id(0) == 0)
    def _():
        part_ref[...] = part

    @pl.when(pl.program_id(0) > 0)
    def _():
        part_ref[...] += part


def local(first, rel_bias, own, behind, ahead, copies):
    tokens, columns = own[0].shape
    heads = columns // HEAD_DIM
    column = pl.BlockSpec((tokens, HEAD_DIM), lambda h: (0, h))

    def halo(n):
        return pl.BlockSpec((WINDOW, HEAD_DIM), lambda h: (0, n * heads + h))

    part = jax.ShapeDtypeStruct((copies, 8, WINDOW), F32)
    return pl.pallas_call(
        local_kernel,
        grid=(heads,),
        in_specs=[scalar_spec(), whole(rel_bias)]
        + [column] * 4
        + [halo(0), halo(1), halo(0), halo(1), halo(2), halo(3)],
        out_specs=[column] * 4 + [whole(part)],
        out_shape=[jax.ShapeDtypeStruct((tokens, columns), BF16)] * 4 + [part],
        name="local",
        compiler_params=PARAMS,
    )(first, rel_bias, *own, behind, behind, ahead, ahead, ahead, ahead)


def shards(
    routed_q,
    routed_k,
    routed_v,
    routed_grad,
    local_q,
    local_k,
    local_v,
    local_grad,
    clusters,
    cluster_slot,
    rel_bias,
):
    ctx_size = lax.axis_size("ctx")
    device_count = ctx_size * lax.axis_size("head")
    tokens = routed_q.shape[0]
    per_source = 2 * tokens // cluster_slot.shape[1]

    heads = cluster_slot.shape[0]
    me = lax.axis_index("ctx").reshape(1, 1)
    in_hbm = lambda arrays: tuple(pltpu.with_memory_space_constraint(a, pltpu.HBM) for a in arrays)
    routed = in_hbm((routed_q, routed_k, routed_v, routed_grad))
    own = in_hbm((local_q, local_k, local_v, local_grad))

    flats, got = [], []
    for head in range(heads):
        flat, chunks = pack(me, clusters, cluster_slot, routed, head, ctx_size, per_source)
        flats.append(flat)
        got.append(exchange(chunks))

    lead, tail = halo_pieces(own)
    behind = lax.ppermute(tail, "ctx", [(i, i + 1) for i in range(ctx_size - 1)])
    ahead = lax.ppermute(lead, "ctx", [(i + 1, i) for i in range(ctx_size - 1)])

    centroids, home = (), []
    for head in range(heads):
        back, *centroids = owner(me, got[head], per_source, head, heads, centroids)
        home.append(exchange(back))
    (centroids,) = centroids

    first = (lax.axis_index("ctx") == 0).astype(jnp.int32).reshape(1, 1)
    local_out, local_dq, local_dk, local_dv, part = local(
        first, rel_bias.reshape(1, WINDOW), own, behind, ahead, device_count
    )
    parts = lax.all_to_all(part, ("ctx", "head"), 0, 0, tiled=True)
    bias_grad = jnp.sum(parts[:, 0], axis=0)

    columns = ()
    for head in range(heads):
        columns = unpack(me, flats[head], home[head], head, heads, columns)
    routed_out, routed_dq, routed_dk, routed_dv = columns
    return (
        routed_out,
        routed_dq,
        routed_dk,
        routed_dv,
        centroids,
        local_out,
        local_dq,
        local_dk,
        local_dv,
        bias_grad,
    )


def solution(mesh):
    return jax.shard_map(
        shards,
        mesh=mesh,
        in_specs=(
            P("ctx", "head"),
            P("ctx", "head"),
            P("ctx", "head"),
            P("ctx", "head"),
            P("ctx", "head"),
            P("ctx", "head"),
            P("ctx", "head"),
            P("ctx", "head"),
            P("head", "ctx"),
            P("head", None),
            P(),
        ),
        out_specs=(
            P("ctx", "head"),
            P("ctx", "head"),
            P("ctx", "head"),
            P("ctx", "head"),
            P("head", "ctx", None),
            P("ctx", "head"),
            P("ctx", "head"),
            P("ctx", "head"),
            P("ctx", "head"),
            P(),
        ),
        check_vma=False,
    )
```

profile of v0, /device:TPU:0, one launch (start us, length us, event | category | flops | bytes accessed | tf_op | source)
XLA Modules:
  0.0 81.3 jit_solution(4749365455838968146)
XLA Ops:
  1.3 2.1 %pack.3 = (f32[8,512]{1,0:T(8,128)S(1)}, bf16[128,512]{1,0:T(8,128)(2,1)S(1)}, bf16[128,512]{1,0:T(8,128)(2,1)S(1)}, bf16[128,512]{1,0:T(8,128)(2,1)S(1)}, bf16[...) custom-call(s32[1,1]{1,0:T(1,128)} %bitcast.refs_0_, ...), custom_call_target="tpu_custom_call" | custom-call | tf_op jit(solution)/shard_map/pack/pallas_call | solution.py:92
  3.5 3.1 %collective-permute-start.10 = (bf16[128,512]{1,0:T(8,128)(2,1)S(1)}, bf16[128,512]{1,0:T(8,128)(2,1)S(1)}, u32[]{:S(2)}, u32[]{:S(2)}) collective-permute-start(bf16[128,512]{1,0:T(8,128)(2,1)S(1)} %get-tuple-element.74), channel_id=1, source_target_pairs={{0,16},{4,20},{8,24},{12,28},{16,0},{20,4},{24,8},{28,12},{1,17},{... | collective-permute-start | bytes 393224 | tf_op jit(solution)/shard_map/ppermute | solution.py:210
  6.6 2.1 %collective-permute-start.12 = (bf16[128,512]{1,0:T(8,128)(2,1)S(1)}, bf16[128,512]{1,0:T(8,128)(2,1)S(1)}, u32[]{:S(2)}, u32[]{:S(2)}) collective-permute-start(bf16[128,512]{1,0:T(8,128)(2,1)S(1)} %get-tuple-element.76), channel_id=1, source_target_pairs={{0,24},{4,28},{8,16},{12,20},{16,8},{20,12},{24,0},{28,4},{1,25},{... | collective-permute-start | bytes 393224 | tf_op jit(solution)/shard_map/ppermute | solution.py:210
  9.6 6.3 %collective-permute-done.10.refs_5_ = bf16[128,512]{1,0:T(8,128)(2,1)S(1)} collective-permute-done((bf16[128,512]{1,0:T(8,128)(2,1)S(1)}, bf16[128,512]{1,0:T(8,128)(2,1)S(1)}, u32[]{:S(2)}, u32[]{:S(2)}) %collective-permute-start.10) | collective-permute-done | bytes 131104 | tf_op jit(solution)/shard_map/ppermute | solution.py:210
  15.9 2.1 %collective-permute-start.8 = (bf16[128,512]{1,0:T(8,128)(2,1)S(1)}, bf16[128,512]{1,0:T(8,128)(2,1)S(1)}, u32[]{:S(2)}, u32[]{:S(2)}) collective-permute-start(bf16[128,512]{1,0:T(8,128)(2,1)S(1)} %get-tuple-element.72), channel_id=1, source_target_pairs={{0,8},{4,12},{8,0},{12,4},{16,24},{20,28},{24,16},{28,20},{1,9},{5... | collective-permute-start | bytes 393224 | tf_op jit(solution)/shard_map/ppermute | solution.py:210
  18.1 2.2 %pack.2 = (f32[8,512]{1,0:T(8,128)S(1)}, bf16[128,512]{1,0:T(8,128)(2,1)S(1)}, bf16[128,512]{1,0:T(8,128)(2,1)S(1)}, bf16[128,512]{1,0:T(8,128)(2,1)S(1)}, bf16[...) custom-call(s32[1,1]{1,0:T(1,128)} %bitcast.refs_0_, ...), custom_call_target="tpu_custom_call" | custom-call | tf_op jit(solution)/shard_map/pack/pallas_call | solution.py:92
  20.4 2.0 %collective-permute-start.1 = (bf16[128,512]{1,0:T(8,128)(2,1)S(1)}, bf16[128,512]{1,0:T(8,128)(2,1)S(1)}, u32[]{:S(2)}, u32[]{:S(2)}) collective-permute-start(bf16[128,512]{1,0:T(8,128)(2,1)S(1)} %get-tuple-element.64), channel_id=1, source_target_pairs={{0,8},{4,12},{8,0},{12,4},{16,24},{20,28},{24,16},{28,20},{1,9},{5... | collective-permute-start | bytes 393224 | tf_op jit(solution)/shard_map/ppermute | solution.py:210
  22.5 2.0 %collective-permute-start.3 = (bf16[128,512]{1,0:T(8,128)(2,1)S(1)}, bf16[128,512]{1,0:T(8,128)(2,1)S(1)}, u32[]{:S(2)}, u32[]{:S(2)}) collective-permute-start(bf16[128,512]{1,0:T(8,128)(2,1)S(1)} %get-tuple-element.66), channel_id=1, source_target_pairs={{0,16},{4,20},{8,24},{12,28},{16,0},{20,4},{24,8},{28,12},{1,17},{... | collective-permute-start | bytes 393224 | tf_op jit(solution)/shard_map/ppermute | solution.py:210
  26.0 2.5 %collective-permute-start.5 = (bf16[128,512]{1,0:T(8,128)(2,1)S(1)}, bf16[128,512]{1,0:T(8,128)(2,1)S(1)}, u32[]{:S(2)}, u32[]{:S(2)}) collective-permute-start(bf16[128,512]{1,0:T(8,128)(2,1)S(1)} %get-tuple-element.68), channel_id=1, source_target_pairs={{0,24},{4,28},{8,16},{12,20},{16,8},{20,12},{24,0},{28,4},{1,25},{... | collective-permute-start | bytes 393224 | tf_op jit(solution)/shard_map/ppermute | solution.py:210
  28.5 2.0 %collective-permute-start.6 = (bf16[128,512]{1,0:T(8,128)(2,1)S(1)}, bf16[128,512]{1,0:T(8,128)(2,1)S(1)}, u32[]{:S(2)}, u32[]{:S(2)}) collective-permute-start(bf16[128,512]{1,0:T(8,128)(2,1)S(1)} %get-tuple-element.69), channel_id=1, source_target_pairs={{0,28},{4,24},{8,20},{12,16},{16,12},{20,8},{24,4},{28,0},{1,29},{... | collective-permute-start | bytes 393224 | tf_op jit(solution)/shard_map/ppermute | solution.py:210
  30.5 2.4 %collective-permute-start.28 = (bf16[128,512]{1,0:T(8,128)(2,1)S(1)}, bf16[128,512]{1,0:T(8,128)(2,1)S(1)}, u32[]{:S(2)}, u32[]{:S(2)}) collective-permute-start(bf16[128,512]{1,0:T(8,128)(2,1)S(1)} %get-tuple-element.105), channel_id=1, source_target_pairs={{0,4},{4,8},{8,12},{12,16},{16,20},{20,24},{24,28},{1,5},{5,9},{9,... | collective-permute-start | bytes 393224 | tf_op jit(solution)/shard_map/ppermute | solution.py:372
  34.2 1.6 %owner.2 = (bf16[128,512]{1,0:T(8,128)(2,1)S(1)}, bf16[128,512]{1,0:T(8,128)(2,1)S(1)}, bf16[128,512]{1,0:T(8,128)(2,1)S(1)}, bf16[128,512]{1,0:T(8,128)(2,1)S(1...) custom-call(s32[1,1]{1,0:T(1,128)} %bitcast.refs_0_, ...), custom_call_target="tpu_custom_call" | custom-call | tf_op jit(solution)/shard_map/owner/pallas_call | solution.py:155
  37.2 3.2 %collective-permute-start.22 = (bf16[128,512]{1,0:T(8,128)(2,1)S(1)}, bf16[128,512]{1,0:T(8,128)(2,1)S(1)}, u32[]{:S(2)}, u32[]{:S(2)}) collective-permute-start(bf16[128,512]{1,0:T(8,128)(2,1)S(1)} %get-tuple-element.90), channel_id=1, source_target_pairs={{0,8},{4,12},{8,0},{12,4},{16,24},{20,28},{24,16},{28,20},{1,9},{5... | collective-permute-start | bytes 393224 | tf_op jit(solution)/shard_map/ppermute | solution.py:210
  40.5 2.9 %collective-permute-start.24 = (bf16[128,512]{1,0:T(8,128)(2,1)S(1)}, bf16[128,512]{1,0:T(8,128)(2,1)S(1)}, u32[]{:S(2)}, u32[]{:S(2)}) collective-permute-start(bf16[128,512]{1,0:T(8,128)(2,1)S(1)} %get-tuple-element.92), channel_id=1, source_target_pairs={{0,16},{4,20},{8,24},{12,28},{16,0},{20,4},{24,8},{28,12},{1,17},{... | collective-permute-start | bytes 393224 | tf_op jit(solution)/shard_map/ppermute | solution.py:210
  43.4 1.6 %owner.3 = (bf16[128,512]{1,0:T(8,128)(2,1)S(1)}, bf16[128,512]{1,0:T(8,128)(2,1)S(1)}, bf16[128,512]{1,0:T(8,128)(2,1)S(1)}, bf16[128,512]{1,0:T(8,128)(2,1)S(1...) custom-call(s32[1,1]{1,0:T(1,128)} %bitcast.refs_0_, ...), custom_call_target="tpu_custom_call", output_to_operand_aliasing={{8}: (9, {})} | custom-call | tf_op jit(solution)/shard_map/owner/pallas_call | solution.py:155
  45.3 4.5 %collective-permute-start.26 = (bf16[128,512]{1,0:T(8,128)(2,1)S(1)}, bf16[128,512]{1,0:T(8,128)(2,1)S(1)}, u32[]{:S(2)}, u32[]{:S(2)}) collective-permute-start(bf16[128,512]{1,0:T(8,128)(2,1)S(1)} %get-tuple-element.94), channel_id=1, source_target_pairs={{0,24},{4,28},{8,16},{12,20},{16,8},{20,12},{24,0},{28,4},{1,25},{... | collective-permute-start | bytes 393224 | tf_op jit(solution)/shard_map/ppermute | solution.py:210
  49.9 2.2 %collective-permute-start.27 = (bf16[128,512]{1,0:T(8,128)(2,1)S(1)}, bf16[128,512]{1,0:T(8,128)(2,1)S(1)}, u32[]{:S(2)}, u32[]{:S(2)}) collective-permute-start(bf16[128,512]{1,0:T(8,128)(2,1)S(1)} %get-tuple-element.95), channel_id=1, source_target_pairs={{0,28},{4,24},{8,20},{12,16},{16,12},{20,8},{24,4},{28,0},{1,29},{... | collective-permute-start | bytes 393224 | tf_op jit(solution)/shard_map/ppermute | solution.py:210
  53.0 4.5 %local.1 = (bf16[512,256]{1,0:T(8,128)(2,1)}, bf16[512,256]{1,0:T(8,128)(2,1)}, bf16[512,256]{1,0:T(8,128)(2,1)}, bf16[512,256]{1,0:T(8,128)(2,1)}, f32[32,8,128]{2,1,0:T(8,128)}) custom-call(s32[1,1]{1,0:T(1,128)} %bitcast.1.first_ref, f32[1,128]{1,0:T(1,128)S(1)} %bitcast.3, bf16[512,256]{1,0:T(8,128)(2,1)} %q_ref.1, bf16[512,256]{1,0:T(8,128)(2,1)} %k_ref.1, ...), custom_call_target="tpu_custom_call" | custom-call | tf_op jit(solution)/shard_map/local/pallas_call | solution.py:328
  57.6 5.3 %all-to-all-start = ((f32[32,8,128]{2,1,0:T(8,128)}), f32[32,8,128]{2,1,0:T(8,128)S(1)}, u32[]{:S(2)}, u32[]{:S(2)}) async-start(f32[32,8,128]{2,1,0:T(8,128)} %get-tuple-element.111), calls=%async_computation | async-start | bytes 262144 | tf_op jit(solution)/shard_map/all_to_all | solution.py:385
  62.9 1.6 %collective-permute-start.16 = (bf16[128,512]{1,0:T(8,128)(2,1)S(1)}, bf16[128,512]{1,0:T(8,128)(2,1)S(1)}, u32[]{:S(2)}, u32[]{:S(2)}) collective-permute-start(bf16[128,512]{1,0:T(8,128)(2,1)S(1)} %get-tuple-element.82), channel_id=1, source_target_pairs={{0,12},{4,8},{8,4},{12,0},{16,28},{20,24},{24,20},{28,16},{1,13},{... | collective-permute-start | bytes 393224 | tf_op jit(solution)/shard_map/ppermute | solution.py:210
  68.8 1.5 %unpack.2 = (bf16[512,256]{1,0:T(8,128)(2,1)}, bf16[512,256]{1,0:T(8,128)(2,1)}, bf16[512,256]{1,0:T(8,128)(2,1)}, bf16[512,256]{1,0:T(8,128)(2,1)}) custom-call(s32[1,1]{1,0:T(1,128)} %bitcast.refs_0_, f32[8,512]{1,0:T(8,128)S(1)} %get-tuple-element.87.refs_1_, bf16[128,512]{1,0:T(8,128)(2,1)S(1)} %get-tuple-element.88.refs_2_, ...), custom_call_target="tpu_custom_call" | custom-call | tf_op jit(solution)/shard_map/unpack/pallas_call | solution.py:194
  70.4 6.7 %collective-permute-done.17.refs_6_ = bf16[128,512]{1,0:T(8,128)(2,1)S(1)} collective-permute-done((bf16[128,512]{1,0:T(8,128)(2,1)S(1)}, bf16[128,512]{1,0:T(8,128)(2,1)S(1)}, u32[]{:S(2)}, u32[]{:S(2)}) %collective-permute-start.17) | collective-permute-done | bytes 131104 | tf_op jit(solution)/shard_map/ppermute | solution.py:210
  77.1 2.1 %collective-permute-done.18.refs_7_ = bf16[128,512]{1,0:T(8,128)(2,1)S(1)} collective-permute-done((bf16[128,512]{1,0:T(8,128)(2,1)S(1)}, bf16[128,512]{1,0:T(8,128)(2,1)S(1)}, u32[]{:S(2)}, u32[]{:S(2)}) %collective-permute-start.18) | collective-permute-done | bytes 131104 | tf_op jit(solution)/shard_map/ppermute | solution.py:210
  79.2 1.5 %unpack.3 = (bf16[512,256]{1,0:T(8,128)(2,1)}, bf16[512,256]{1,0:T(8,128)(2,1)}, bf16[512,256]{1,0:T(8,128)(2,1)}, bf16[512,256]{1,0:T(8,128)(2,1)}) custom-call(s32[1,1]{1,0:T(1,128)} %bitcast.refs_0_, f32[8,512]{1,0:T(8,128)S(1)} %get-tuple-element.61.refs_1_, ...), custom_call_target="tpu_custom_call", output_to_operand_aliasing={{0}: (10, {}), {1}: (11, {}), {2}: (12, {}), {3}: (13, {})} | custom-call | tf_op jit(solution)/shard_map/unpack/pallas_call | solution.py:194
  (53 shorter events, 12.2 us)
Async XLA Ops:
  3.5 12.4 %collective-permute-start.10 = (bf16[128,512]{1,0:T(8,128)(2,1)S(1)}, bf16[128,512]{1,0:T(8,128)(2,1)S(1)}, u32[]{:S(2)}, u32[]{:S(2)}) collective-permute-start(bf16[128,512]{1,0:T(8,128)(2,1)S(1)} %get-tuple-element.74), channel_id=1, source_target_pairs={{0,16},{4,20},{8,24},{12,28},{16,0},{20,4},{24,8},{28,12},{1,17},{... | collective-permute-start | bytes 393224 | tf_op jit(solution)/shard_map/ppermute | solution.py:210
  6.6 13.7 %collective-permute-start.11 = (bf16[128,512]{1,0:T(8,128)(2,1)S(1)}, bf16[128,512]{1,0:T(8,128)(2,1)S(1)}, u32[]{:S(2)}, u32[]{:S(2)}) collective-permute-start(bf16[128,512]{1,0:T(8,128)(2,1)S(1)} %get-tuple-element.75), channel_id=1, source_target_pairs={{0,20},{4,16},{8,28},{12,24},{16,4},{20,0},{24,12},{28,8},{1,21},{... | collective-permute-start | bytes 393224 | tf_op jit(solution)/shard_map/ppermute | solution.py:210
  6.6 13.7 %collective-permute-start.12 = (bf16[128,512]{1,0:T(8,128)(2,1)S(1)}, bf16[128,512]{1,0:T(8,128)(2,1)S(1)}, u32[]{:S(2)}, u32[]{:S(2)}) collective-permute-start(bf16[128,512]{1,0:T(8,128)(2,1)S(1)} %get-tuple-element.76), channel_id=1, source_target_pairs={{0,24},{4,28},{8,16},{12,20},{16,8},{20,12},{24,0},{28,4},{1,25},{... | collective-permute-start | bytes 393224 | tf_op jit(solution)/shard_map/ppermute | solution.py:210
  8.7 11.7 %collective-permute-start.13 = (bf16[128,512]{1,0:T(8,128)(2,1)S(1)}, bf16[128,512]{1,0:T(8,128)(2,1)S(1)}, u32[]{:S(2)}, u32[]{:S(2)}) collective-permute-start(bf16[128,512]{1,0:T(8,128)(2,1)S(1)} %get-tuple-element.77), channel_id=1, source_target_pairs={{0,28},{4,24},{8,20},{12,16},{16,12},{20,8},{24,4},{28,0},{1,29},{... | collective-permute-start | bytes 393224 | tf_op jit(solution)/shard_map/ppermute | solution.py:210
  9.2 13.2 %collective-permute-start.7 = (bf16[128,512]{1,0:T(8,128)(2,1)S(1)}, bf16[128,512]{1,0:T(8,128)(2,1)S(1)}, u32[]{:S(2)}, u32[]{:S(2)}) collective-permute-start(bf16[128,512]{1,0:T(8,128)(2,1)S(1)} %get-tuple-element.71), channel_id=1, source_target_pairs={{0,4},{4,0},{8,12},{12,8},{16,20},{20,16},{24,28},{28,24},{1,5},{5... | collective-permute-start | bytes 393224 | tf_op jit(solution)/shard_map/ppermute | solution.py:210
  22.5 10.5 %collective-permute-start.3 = (bf16[128,512]{1,0:T(8,128)(2,1)S(1)}, bf16[128,512]{1,0:T(8,128)(2,1)S(1)}, u32[]{:S(2)}, u32[]{:S(2)}) collective-permute-start(bf16[128,512]{1,0:T(8,128)(2,1)S(1)} %get-tuple-element.66), channel_id=1, source_target_pairs={{0,16},{4,20},{8,24},{12,28},{16,0},{20,4},{24,8},{28,12},{1,17},{... | collective-permute-start | bytes 393224 | tf_op jit(solution)/shard_map/ppermute | solution.py:210
  25.5 10.5 %collective-permute-start.4 = (bf16[128,512]{1,0:T(8,128)(2,1)S(1)}, bf16[128,512]{1,0:T(8,128)(2,1)S(1)}, u32[]{:S(2)}, u32[]{:S(2)}) collective-permute-start(bf16[128,512]{1,0:T(8,128)(2,1)S(1)} %get-tuple-element.67), channel_id=1, source_target_pairs={{0,20},{4,16},{8,28},{12,24},{16,4},{20,0},{24,12},{28,8},{1,21},{... | collective-permute-start | bytes 393224 | tf_op jit(solution)/shard_map/ppermute | solution.py:210
  26.0 11.2 %collective-permute-start.5 = (bf16[128,512]{1,0:T(8,128)(2,1)S(1)}, bf16[128,512]{1,0:T(8,128)(2,1)S(1)}, u32[]{:S(2)}, u32[]{:S(2)}) collective-permute-start(bf16[128,512]{1,0:T(8,128)(2,1)S(1)} %get-tuple-element.68), channel_id=1, source_target_pairs={{0,24},{4,28},{8,16},{12,20},{16,8},{20,12},{24,0},{28,4},{1,25},{... | collective-permute-start | bytes 393224 | tf_op jit(solution)/shard_map/ppermute | solution.py:210
  28.5 12.0 %collective-permute-start.6 = (bf16[128,512]{1,0:T(8,128)(2,1)S(1)}, bf16[128,512]{1,0:T(8,128)(2,1)S(1)}, u32[]{:S(2)}, u32[]{:S(2)}) collective-permute-start(bf16[128,512]{1,0:T(8,128)(2,1)S(1)} %get-tuple-element.69), channel_id=1, source_target_pairs={{0,28},{4,24},{8,20},{12,16},{16,12},{20,8},{24,4},{28,0},{1,29},{... | collective-permute-start | bytes 393224 | tf_op jit(solution)/shard_map/ppermute | solution.py:210
  30.5 9.9 %collective-permute-start.28 = (bf16[128,512]{1,0:T(8,128)(2,1)S(1)}, bf16[128,512]{1,0:T(8,128)(2,1)S(1)}, u32[]{:S(2)}, u32[]{:S(2)}) collective-permute-start(bf16[128,512]{1,0:T(8,128)(2,1)S(1)} %get-tuple-element.105), channel_id=1, source_target_pairs={{0,4},{4,8},{8,12},{12,16},{16,20},{20,24},{24,28},{1,5},{5,9},{9,... | collective-permute-start | bytes 393224 | tf_op jit(solution)/shard_map/ppermute | solution.py:372
  32.9 19.2 %collective-permute-start.29 = (bf16[128,1024]{1,0:T(8,128)(2,1)S(1)}, bf16[128,1024]{1,0:T(8,128)(2,1)S(1)}, u32[]{:S(2)}, u32[]{:S(2)}) collective-permute-start(bf16[128,1024]{1,0:T(8,128)(2,1)S(1)} %get-tuple-element.106), channel_id=1, source_target_pairs={{4,0},{8,4},{12,8},{16,12},{20,16},{24,20},{28,24},{5,1},{9,5},{13... | collective-permute-start | bytes 786440 | tf_op jit(solution)/shard_map/ppermute | solution.py:373
  36.1 8.9 %collective-permute-start.21 = (bf16[128,512]{1,0:T(8,128)(2,1)S(1)}, bf16[128,512]{1,0:T(8,128)(2,1)S(1)}, u32[]{:S(2)}, u32[]{:S(2)}) collective-permute-start(bf16[128,512]{1,0:T(8,128)(2,1)S(1)} %get-tuple-element.89), channel_id=1, source_target_pairs={{0,4},{4,0},{8,12},{12,8},{16,20},{20,16},{24,28},{28,24},{1,5},{5... | collective-permute-start | bytes 393224 | tf_op jit(solution)/shard_map/ppermute | solution.py:210
  40.5 9.4 %collective-permute-start.23 = (bf16[128,512]{1,0:T(8,128)(2,1)S(1)}, bf16[128,512]{1,0:T(8,128)(2,1)S(1)}, u32[]{:S(2)}, u32[]{:S(2)}) collective-permute-start(bf16[128,512]{1,0:T(8,128)(2,1)S(1)} %get-tuple-element.91), channel_id=1, source_target_pairs={{0,12},{4,8},{8,4},{12,0},{16,28},{20,24},{24,20},{28,16},{1,13},{... | collective-permute-start | bytes 393224 | tf_op jit(solution)/shard_map/ppermute | solution.py:210
  40.5 11.7 %collective-permute-start.24 = (bf16[128,512]{1,0:T(8,128)(2,1)S(1)}, bf16[128,512]{1,0:T(8,128)(2,1)S(1)}, u32[]{:S(2)}, u32[]{:S(2)}) collective-permute-start(bf16[128,512]{1,0:T(8,128)(2,1)S(1)} %get-tuple-element.92), channel_id=1, source_target_pairs={{0,16},{4,20},{8,24},{12,28},{16,0},{20,4},{24,8},{28,12},{1,17},{... | collective-permute-start | bytes 393224 | tf_op jit(solution)/shard_map/ppermute | solution.py:210
  45.0 17.9 %collective-permute-start.25 = (bf16[128,512]{1,0:T(8,128)(2,1)S(1)}, bf16[128,512]{1,0:T(8,128)(2,1)S(1)}, u32[]{:S(2)}, u32[]{:S(2)}) collective-permute-start(bf16[128,512]{1,0:T(8,128)(2,1)S(1)} %get-tuple-element.93), channel_id=1, source_target_pairs={{0,20},{4,16},{8,28},{12,24},{16,4},{20,0},{24,12},{28,8},{1,21},{... | collective-permute-start | bytes 393224 | tf_op jit(solution)/shard_map/ppermute | solution.py:210
  45.3 19.1 %collective-permute-start.26 = (bf16[128,512]{1,0:T(8,128)(2,1)S(1)}, bf16[128,512]{1,0:T(8,128)(2,1)S(1)}, u32[]{:S(2)}, u32[]{:S(2)}) collective-permute-start(bf16[128,512]{1,0:T(8,128)(2,1)S(1)} %get-tuple-element.94), channel_id=1, source_target_pairs={{0,24},{4,28},{8,16},{12,20},{16,8},{20,12},{24,0},{28,4},{1,25},{... | collective-permute-start | bytes 393224 | tf_op jit(solution)/shard_map/ppermute | solution.py:210
  49.9 16.0 %collective-permute-start.27 = (bf16[128,512]{1,0:T(8,128)(2,1)S(1)}, bf16[128,512]{1,0:T(8,128)(2,1)S(1)}, u32[]{:S(2)}, u32[]{:S(2)}) collective-permute-start(bf16[128,512]{1,0:T(8,128)(2,1)S(1)} %get-tuple-element.95), channel_id=1, source_target_pairs={{0,28},{4,24},{8,20},{12,16},{16,12},{20,8},{24,4},{28,0},{1,29},{... | collective-permute-start | bytes 393224 | tf_op jit(solution)/shard_map/ppermute | solution.py:210
  52.1 14.1 %collective-permute-start.14 = (bf16[128,512]{1,0:T(8,128)(2,1)S(1)}, bf16[128,512]{1,0:T(8,128)(2,1)S(1)}, u32[]{:S(2)}, u32[]{:S(2)}) collective-permute-start(bf16[128,512]{1,0:T(8,128)(2,1)S(1)} %get-tuple-element.80), channel_id=1, source_target_pairs={{0,4},{4,0},{8,12},{12,8},{16,20},{20,16},{24,28},{28,24},{1,5},{5... | collective-permute-start | bytes 393224 | tf_op jit(solution)/shard_map/ppermute | solution.py:210
  52.1 15.5 %collective-permute-start.15 = (bf16[128,512]{1,0:T(8,128)(2,1)S(1)}, bf16[128,512]{1,0:T(8,128)(2,1)S(1)}, u32[]{:S(2)}, u32[]{:S(2)}) collective-permute-start(bf16[128,512]{1,0:T(8,128)(2,1)S(1)} %get-tuple-element.81), channel_id=1, source_target_pairs={{0,8},{4,12},{8,0},{12,4},{16,24},{20,28},{24,16},{28,20},{1,9},{5... | collective-permute-start | bytes 393224 | tf_op jit(solution)/shard_map/ppermute | solution.py:210
  57.6 23.2 %all-to-all-start = ((f32[32,8,128]{2,1,0:T(8,128)}), f32[32,8,128]{2,1,0:T(8,128)S(1)}, u32[]{:S(2)}, u32[]{:S(2)}) async-start(f32[32,8,128]{2,1,0:T(8,128)} %get-tuple-element.111), calls=%async_computation | async-start | bytes 262144 | tf_op jit(solution)/shard_map/all_to_all | solution.py:385
  64.4 12.7 %collective-permute-start.17 = (bf16[128,512]{1,0:T(8,128)(2,1)S(1)}, bf16[128,512]{1,0:T(8,128)(2,1)S(1)}, u32[]{:S(2)}, u32[]{:S(2)}) collective-permute-start(bf16[128,512]{1,0:T(8,128)(2,1)S(1)} %get-tuple-element.83), channel_id=1, source_target_pairs={{0,16},{4,20},{8,24},{12,28},{16,0},{20,4},{24,8},{28,12},{1,17},{... | collective-permute-start | bytes 393224 | tf_op jit(solution)/shard_map/ppermute | solution.py:210
  65.9 13.3 %collective-permute-start.18 = (bf16[128,512]{1,0:T(8,128)(2,1)S(1)}, bf16[128,512]{1,0:T(8,128)(2,1)S(1)}, u32[]{:S(2)}, u32[]{:S(2)}) collective-permute-start(bf16[128,512]{1,0:T(8,128)(2,1)S(1)} %get-tuple-element.84), channel_id=1, source_target_pairs={{0,20},{4,16},{8,28},{12,24},{16,4},{20,0},{24,12},{28,8},{1,21},{... | collective-permute-start | bytes 393224 | tf_op jit(solution)/shard_map/ppermute | solution.py:210
  66.2 13.0 %collective-permute-start.19 = (bf16[128,512]{1,0:T(8,128)(2,1)S(1)}, bf16[128,512]{1,0:T(8,128)(2,1)S(1)}, u32[]{:S(2)}, u32[]{:S(2)}) collective-permute-start(bf16[128,512]{1,0:T(8,128)(2,1)S(1)} %get-tuple-element.85), channel_id=1, source_target_pairs={{0,24},{4,28},{8,16},{12,20},{16,8},{20,12},{24,0},{28,4},{1,25},{... | collective-permute-start | bytes 393224 | tf_op jit(solution)/shard_map/ppermute | solution.py:210
  67.6 11.6 %collective-permute-start.20 = (bf16[128,512]{1,0:T(8,128)(2,1)S(1)}, bf16[128,512]{1,0:T(8,128)(2,1)S(1)}, u32[]{:S(2)}, u32[]{:S(2)}) collective-permute-start(bf16[128,512]{1,0:T(8,128)(2,1)S(1)} %get-tuple-element.86), channel_id=1, source_target_pairs={{0,28},{4,24},{8,20},{12,16},{16,12},{20,8},{24,4},{28,0},{1,29},{... | collective-permute-start | bytes 393224 | tf_op jit(solution)/shard_map/ppermute | solution.py:210
  (10 other events, 51.3 us)
where the time goes:
time: 81.7 us; the launch traced here: 81.3 us
  starting transfers between devices  46.6 us (57%)
  Pallas kernels  16.1 us (20%)
  waiting for transfers between devices  15.9 us (19%)
  local copies, waits for them, and re-layouts  1.33 us (2%)
    ppermute x28, starting transfers between devices, exchange(): moved[m] = lax.ppermute(chunks[m], 'ctx', [(i, i ^ m) for i in range(size)])  37.7 us
    ppermute x28, waiting for transfers between devices, exchange(): moved[m] = lax.ppermute(chunks[m], 'ctx', [(i, i ^ m) for i in range(size)])  15.9 us
    all_to_all x1, starting transfers between devices, shards(): parts = lax.all_to_all(part, ('ctx', 'head'), 0, 0, tiled=True)  5.28 us
    pallas_call x1, Pallas kernels, local(): pl.pallas_call(local_kernel, grid=(heads,), in_specs=[scalar_spec(), whol...  4.55 us
    pallas_call x2, Pallas kernels, pack(): pl.pallas_call(lambda *refs: pack_kernel(*refs, head=head, per_source=per...  4.3 us
    pallas_call x2, Pallas kernels, owner(): pl.pallas_call(lambda *refs: owner_kernel(*refs, per_source=per_source, s...  3.17 us
    pallas_call x2, Pallas kernels, unpack(): pl.pallas_call(lambda *refs: unpack_kernel(*refs, chunks=len(home)), grid...  3.1 us
    ppermute x1, starting transfers between devices, shards(): lax.ppermute(tail, 'ctx', [(i, i + 1) for i in range(ctx_size - 1)])  2.38 us
  transfers between devices with their start and end apart: 31, of which 5 were waited for; matrix products, arithmetic and copies ran while one was open for 0% of the time, Pallas kernels for 17%

commit v1 on v0

--- a/solution.py
+++ b/solution.py
@@ -43,11 +43,18 @@
     return probs, weighted - probs * jnp.sum(weighted, axis=0, keepdims=True)
 
 
-def pack_kernel(me_ref, ids_ref, slots_ref, q_ref, k_ref, v_ref, g_ref, flat_ref, *out_refs, head, per_source):
+def pack_kernel(me_ref, ids_ref, slots_ref, q_ref, k_ref, v_ref, g_ref, *refs, head, per_source, halo):
+    halo_refs, (flat_ref, *out_refs) = refs[:halo], refs[halo:]
+    if halo:
+        *out_refs, lead_ref, tail_ref = out_refs
+        split = (lead_ref, halo_refs[:4]), (tail_ref, halo_refs[4:])
+        for to_ref, from_refs in split:
+            for n, ref in enumerate(from_refs):
+                to_ref[:, n * ref.shape[1] : (n + 1) * ref.shape[1]] = ref[...]
     ids = ids_ref[head : head + 1, :]
     tokens = ids.shape[1]
     clusters = slots_ref.shape[1]
-    rows = out_refs[0].shape[0]
+    rows = out_refs[0].shape[0] // 2
     member = iota((clusters, tokens), 0) == ids
     member_low = jnp.where(member, 1.0, 0.0).astype(BF16)
     earlier = jnp.where(iota((tokens, tokens), 0) < iota((tokens, tokens), 1), 1.0, 0.0).astype(BF16)
@@ -61,16 +68,18 @@
     dim = k_ref.shape[1]
     me = me_ref[0, 0]
     slot = iota((rows, tokens), 0)
-    chosen = [jnp.where(slot == where_to - (me ^ m) * rows, 1.0, 0.0) for m in range(len(out_refs))]
+    chosen = [jnp.where(slot == where_to - (me ^ m) * rows, 1.0, 0.0) for m in range(2 * len(out_refs))]
     moved = dot_nn(jnp.concatenate([c.astype(BF16) for c in chosen], axis=0), data)
     first_col = iota((rows, dim), 1) == 0
-    for m, out_ref in enumerate(out_refs):
+    for m in range(2 * len(out_refs)):
+        out_ref = out_refs[m // 2]
+        at = slice(m % 2 * rows, (m % 2 + 1) * rows)
         part = moved[m * rows : (m + 1) * rows]
         filled = jnp.sum(chosen[m], axis=1, keepdims=True) > 0.5
         marked = jnp.where(first_col & ~filled, EMPTY, part[:, dim : 2 * dim])
-        out_ref[:, :dim] = part[:, :dim].astype(BF16)
-        out_ref[:, dim : 2 * dim] = marked.astype(BF16)
-        out_ref[:, 2 * dim :] = part[:, 2 * dim :].astype(BF16)
+        out_ref[at, :dim] = part[:, :dim].astype(BF16)
+        out_ref[at, dim : 2 * dim] = marked.astype(BF16)
+        out_ref[at, 2 * dim :] = part[:, 2 * dim :].astype(BF16)
 
 
 def scalar_spec():
@@ -81,33 +90,42 @@
     return pl.BlockSpec(array.shape, lambda *_: (0,) * array.ndim)
 
 
-def pack(me, ids, slots, arrays, head, dests, per_source):
+def pack(me, ids, slots, arrays, head, dests, per_source, own):
     tokens = arrays[0].shape[0]
     clusters = slots.shape[1]
     rows = clusters * per_source // dests
     width = len(arrays) * HEAD_DIM
     column = pl.BlockSpec((tokens, HEAD_DIM), lambda i: (0, head))
     shapes = [jax.ShapeDtypeStruct((8, tokens), F32)]
-    shapes += [jax.ShapeDtypeStruct((rows, width), BF16)] * dests
+    shapes += [jax.ShapeDtypeStruct((2 * rows, width), BF16)] * (dests // 2)
+    operands, specs = [], []
+    if own:
+        columns = own[0].shape[1]
+        first = pl.BlockSpec((WINDOW, columns), lambda i: (0, 0))
+        last = pl.BlockSpec((WINDOW, columns), lambda i: (tokens // WINDOW - 1, 0))
+        operands = [*own, own[1], own[2]]
+        specs = [first] * 4 + [last] * 2
+        shapes += [jax.ShapeDtypeStruct((WINDOW, n * columns), BF16) for n in (4, 2)]
     flat, *chunks = pl.pallas_call(
-        lambda *refs: pack_kernel(*refs, head=head, per_source=per_source),
+        lambda *refs: pack_kernel(*refs, head=head, per_source=per_source, halo=len(operands)),
         grid=(1,),
-        in_specs=[scalar_spec(), whole(ids), whole(slots)] + [column] * 4,
+        in_specs=[scalar_spec(), whole(ids), whole(slots)] + [column] * 4 + specs,
         out_specs=[whole(s) for s in shapes],
         out_shape=shapes,
         name="pack",
         compiler_params=PARAMS,
-    )(me, ids, slots, *arrays)
+    )(me, ids, slots, *arrays, *operands)
     return flat, chunks
 
 
 def owner_kernel(me_ref, *refs, per_source, sources):
     got_refs = refs[:sources]
-    out_refs = refs[-sources - 1 : -1]
+    out_refs = refs[-sources // 2 - 1 : -1]
     centroid_ref = refs[-1]
     dim = HEAD_DIM
     capacity = sources * per_source
-    clusters = got_refs[0].shape[0] // per_source
+    rows = got_refs[0].shape[0] // 2
+    clusters = rows // per_source
     key = iota((capacity, capacity), 0)
     query = iota((capacity, capacity), 1)
     base = me_ref[0, 0] * per_source
@@ -115,17 +133,26 @@
     diagonal = key == query
     first_col = iota((capacity, dim), 1) == 0
     scaling = dim ** (-0.5)
-    spots = [slice(c * per_source, (c + 1) * per_source) for c in range(clusters)]
+    spots = [c * per_source for c in range(clusters)]
 
     def gathered(part):
         at = slice(part * dim, (part + 1) * dim)
-        return [jnp.concatenate([ref[spot, at] for ref in got_refs], axis=0) for spot in spots]
+        return [
+            jnp.concatenate(
+                [ref[m % 2 * rows + spot : m % 2 * rows + spot + per_source, at] for m, ref in enumerate(got_refs)],
+                axis=0,
+            )
+            for spot in spots
+        ]
 
     def scatter(part, results):
         at = slice(part * dim, (part + 1) * dim)
         for spot, result in zip(spots, results):
-            for m, ref in enumerate(out_refs):
-                ref[spot, at] = result[m * per_source : (m + 1) * per_source].astype(BF16)
+            for m in range(sources):
+                to = m % 2 * rows + spot
+                out_refs[m // 2][to : to + per_source, at] = result[
+                    m * per_source : (m + 1) * per_source
+                ].astype(BF16)
 
     queries, keys, values, cots = (gathered(part) for part in range(4))
     scores, sums = [], []
@@ -149,8 +176,8 @@
 
 def owner(me, got, per_source, head, heads, previous):
     rows, width = got[0].shape
-    shapes = [jax.ShapeDtypeStruct((rows, width), BF16)] * len(got)
-    held = jax.ShapeDtypeStruct((heads, rows // per_source, HEAD_DIM), F32)
+    shapes = [jax.ShapeDtypeStruct((rows, width), BF16)] * (len(got) // 2)
+    held = jax.ShapeDtypeStruct((heads, rows // 2 // per_source, HEAD_DIM), F32)
     any_spec = pl.BlockSpec(memory_space=pl.ANY)
     *back, centroids = pl.pallas_call(
         lambda *refs: owner_kernel(*refs, per_source=per_source, sources=len(got)),
@@ -159,7 +186,7 @@
         out_specs=[whole(s) for s in shapes]
         + [pl.BlockSpec((1,) + held.shape[1:], lambda i: (head, 0, 0))],
         out_shape=shapes + [held],
-        input_output_aliases={1 + len(got) + n: len(got) + n for n in range(len(previous))},
+        input_output_aliases={1 + len(got) + n: len(shapes) + n for n in range(len(previous))},
         name="owner",
         compiler_params=PARAMS,
     )(me, *got, *previous)
@@ -171,7 +198,7 @@
     width = home_refs[0].shape[1]
     out_refs = refs[-(width // HEAD_DIM) :]
     tokens = flat_ref.shape[1]
-    rows = home_refs[0].shape[0]
+    rows = home_refs[0].shape[0] // 2
     wide = jnp.broadcast_to(flat_ref[:1, :], (HEAD_DIM, tokens)).T.astype(jnp.int32)[:, :rows]
     lane = iota((tokens, rows), 1)
     chosen = jnp.concatenate(
@@ -181,7 +208,9 @@
         ],
         axis=1,
     )
-    home = jnp.concatenate([ref[...] for ref in home_refs], axis=0)
+    home = jnp.concatenate(
+        [ref[m % 2 * rows : (m % 2 + 1) * rows] for m, ref in enumerate(home_refs)], axis=0
+    )
     moved = dot_nn(chosen, home).astype(BF16)
     for n, out_ref in enumerate(out_refs):
         out_ref[...] = moved[:, n * HEAD_DIM : (n + 1) * HEAD_DIM]
@@ -203,12 +232,20 @@
     )(me, flat, *home, *previous)
 
 
-def exchange(chunks):
-    size = len(chunks)
-    moved = [chunks[0]] + [None] * (size - 1)
-    for m in reversed(range(1, size)):
-        moved[m] = lax.ppermute(chunks[m], "ctx", [(i, i ^ m) for i in range(size)])
-    return moved
+def swap(array, mask):
+    size = lax.axis_size("ctx")
+    return lax.ppermute(array, "ctx", [(i, i ^ mask) for i in range(size)])
+
+
+def send_far(pairs):
+    far = [swap(pair, 2 * p) for p, pair in list(enumerate(pairs))[:0:-1]]
+    return pairs[:1] + far[::-1]
+
+
+def send_near(pairs):
+    near = [swap(pairs[0], 1)]
+    near += [swap(pair, 1) for pair in pairs[1:]]
+    return [array for both in zip(pairs, near) for array in both]
 
 
 def shift_rows(array, sign):
@@ -220,30 +257,6 @@
         array = jnp.where((row & step) != 0, rolled, array)
         step *= 2
     return array
-
-
-def halo_kernel(hq_ref, hk_ref, hv_ref, hg_ref, tk_ref, tv_ref, lead_ref, tail_ref):
-    width = hq_ref.shape[1]
-    for n, ref in enumerate((hq_ref, hk_ref, hv_ref, hg_ref)):
-        lead_ref[:, n * width : (n + 1) * width] = ref[...]
-    for n, ref in enumerate((tk_ref, tv_ref)):
-        tail_ref[:, n * width : (n + 1) * width] = ref[...]
-
-
-def halo_pieces(own):
-    tokens, width = own[0].shape
-    head = pl.BlockSpec((WINDOW, width), lambda i: (0, 0))
-    last = pl.BlockSpec((WINDOW, width), lambda i: (tokens // WINDOW - 1, 0))
-    shapes = [jax.ShapeDtypeStruct((WINDOW, n * width), BF16) for n in (4, 2)]
-    return pl.pallas_call(
-        halo_kernel,
-        grid=(1,),
-        in_specs=[head] * 4 + [last] * 2,
-        out_specs=[whole(s) for s in shapes],
-        out_shape=shapes,
-        name="halo",
-        compiler_params=PARAMS,
-    )(*own, own[1], own[2])
 
 
 def local_kernel(
@@ -361,21 +374,28 @@
     in_hbm = lambda arrays: tuple(pltpu.with_memory_space_constraint(a, pltpu.HBM) for a in arrays)
     routed = in_hbm((routed_q, routed_k, routed_v, routed_grad))
     own = in_hbm((local_q, local_k, local_v, local_grad))
+    clusters, cluster_slot = in_hbm((clusters, cluster_slot))
 
     flats, got = [], []
     for head in range(heads):
-        flat, chunks = pack(me, clusters, cluster_slot, routed, head, ctx_size, per_source)
+        ends = own if head == heads - 1 else ()
+        flat, chunks = pack(
+            me, clusters, cluster_slot, routed, head, ctx_size, per_source, ends
+        )
         flats.append(flat)
-        got.append(exchange(chunks))
-
-    lead, tail = halo_pieces(own)
+        if ends:
+            *chunks, lead, tail = chunks
+        got.append(send_far(chunks))
+    got = [send_near(pairs) for pairs in got]
+
     behind = lax.ppermute(tail, "ctx", [(i, i + 1) for i in range(ctx_size - 1)])
     ahead = lax.ppermute(lead, "ctx", [(i + 1, i) for i in range(ctx_size - 1)])
 
     centroids, home = (), []
     for head in range(heads):
         back, *centroids = owner(me, got[head], per_source, head, heads, centroids)
-        home.append(exchange(back))
+        home.append(send_far(back))
+    home = [send_near(pairs) for pairs in home]
     (centroids,) = centroids
 
     first = (lax.axis_index("ctx") == 0).astype(jnp.int32).reshape(1, 1)

time: 81.7 us -> 85.8 us (1.050)
  waiting for transfers between devices: 15.9 us -> 30.1 us
  starting transfers between devices: 46.6 us -> 35.7 us
  other arithmetic: 0.56 us -> 1.46 us
    ppermute x28, starting transfers between devices: 37.7 us -> 26.2 us  [swap(): return lax.ppermute(array, 'ctx', [(i, i ^ mask) for i in range(size)])]
    ppermute x28, waiting for transfers between devices: 15.9 us -> 23.1 us  [swap(): return lax.ppermute(array, 'ctx', [(i, i ^ mask) for i in range(size)])]
    all_to_all x1, waiting for transfers between devices: 0.01 us -> 7.05 us  [shards(): parts = lax.all_to_all(part, ('ctx', 'head'), 0, 0, tiled=True)]
    pallas_call x2, Pallas kernels: 3.1 us -> 4.23 us  [unpack(): pl.pallas_call(lambda *refs: unpack_kernel(*refs, chunks=len(home)), grid...]
    pallas_call x1 -> x0, Pallas kernels: 1.03 us -> none  [halo_pieces(): pl.pallas_call(halo_kernel, grid=(1,), in_specs=[head] * 4 + [last] * 2,...]
    reduce_sum x1, other arithmetic: 0.56 us -> 1.46 us  [shards(): bias_grad = jnp.sum(parts[:, 0], axis=0)]
  transfers between devices with their start and end apart: 31 -> 31, of which waited for: 5 -> 7; matrix products, arithmetic and copies ran while one was open for 0% -> 2% of each run, Pallas kernels for 17% -> 14%
where the time goes in v1:
time: 85.8 us; the launch traced here: 85.5 us
  starting transfers between devices  35.7 us (42%)
  waiting for transfers between devices  30.1 us (35%)
  Pallas kernels  16.8 us (20%)
  other arithmetic  1.46 us (2%)
    ppermute x28, starting transfers between devices, swap(): return lax.ppermute(array, 'ctx', [(i, i ^ mask) for i in range(size)])  26.2 us
    ppermute x28, waiting for transfers between devices, swap(): return lax.ppermute(array, 'ctx', [(i, i ^ mask) for i in range(size)])  23.1 us
    all_to_all x1, waiting for transfers between devices, shards(): parts = lax.all_to_all(part, ('ctx', 'head'), 0, 0, tiled=True)  7.05 us
    all_to_all x1, starting transfers between devices, shards(): parts = lax.all_to_all(part, ('ctx', 'head'), 0, 0, tiled=True)  5.8 us
    pallas_call x1, Pallas kernels, local(): pl.pallas_call(local_kernel, grid=(heads,), in_specs=[scalar_spec(), whol...  4.55 us
    pallas_call x2, Pallas kernels, pack(): pl.pallas_call(lambda *refs: pack_kernel(*refs, head=head, per_source=per...  4.5 us
    pallas_call x2, Pallas kernels, unpack(): pl.pallas_call(lambda *refs: unpack_kernel(*refs, chunks=len(home)), grid...  4.23 us
    pallas_call x2, Pallas kernels, owner(): pl.pallas_call(lambda *refs: owner_kernel(*refs, per_source=per_source, s...  3.49 us
  transfers between devices with their start and end apart: 31, of which 7 were waited for; matrix products, arithmetic and copies ran while one was open for 2% of the time, Pallas kernels for 14%

profile of v1, /device:TPU:0, one launch (start us, length us, event | category | flops | bytes accessed | tf_op | source)
XLA Modules:
  0.0 85.5 jit_solution(3404395471890781187)
XLA Ops:
  0.6 2.2 %pack.3 = (f32[8,512]{1,0:T(8,128)S(1)}, bf16[256,512]{1,0:T(8,128)(2,1)S(1)}, bf16[256,512]{1,0:T(8,128)(2,1)S(1)}, bf16[256,512]{1,0:T(8,128)(2,1)S(1)}, bf16[256,512]{1,0:T(8,128)(2,1)S(1)}) custom-call(s32[1,1]{1,0:T(1,128)} %bitcast.refs_0_, s32[2,512]{1,0:T(2,128)} %refs_1_.3, s32[2,64]{1,0:T(2,128)} %refs_2_.3, bf16[512,256]{1,0:T(8,128)(2,1)} %refs_3_.3, ...), custom_call_target="tpu_custom_call" | custom-call | tf_op jit(solution)/shard_map/pack/pallas_call | solution.py:109
  2.9 3.1 %collective-permute-start.10 = (bf16[256,512]{1,0:T(8,128)(2,1)S(1)}, bf16[256,512]{1,0:T(8,128)(2,1)S(1)}, u32[]{:S(2)}, u32[]{:S(2)}) collective-permute-start(bf16[256,512]{1,0:T(8,128)(2,1)S(1)} %get-tuple-element.52), channel_id=1, source_target_pairs={{0,16},{4,20},{8,24},{12,28},{16,0},{20,4},{24,8},{28,12},{1,17},{... | collective-permute-start | bytes 786440 | tf_op jit(solution)/shard_map/ppermute | solution.py:237
  5.9 1.4 %collective-permute-start.12 = (bf16[256,512]{1,0:T(8,128)(2,1)S(1)}, bf16[256,512]{1,0:T(8,128)(2,1)S(1)}, u32[]{:S(2)}, u32[]{:S(2)}) collective-permute-start(bf16[256,512]{1,0:T(8,128)(2,1)S(1)} %get-tuple-element.53), channel_id=1, source_target_pairs={{0,24},{4,28},{8,16},{12,20},{16,8},{20,12},{24,0},{28,4},{1,25},{... | collective-permute-start | bytes 786440 | tf_op jit(solution)/shard_map/ppermute | solution.py:237
  7.5 2.3 %pack.2 = (f32[8,512]{1,0:T(8,128)S(1)}, bf16[256,512]{1,0:T(8,128)(2,1)S(1)}, bf16[256,512]{1,0:T(8,128)(2,1)S(1)}, bf16[256,512]{1,0:T(8,128)(2,1)S(1)}, bf16[...) custom-call(s32[1,1]{1,0:T(1,128)} %bitcast.refs_0_, s32[2,512]{1,0:T(2,128)} %refs_1_.3, ...), custom_call_target="tpu_custom_call" | custom-call | tf_op jit(solution)/shard_map/pack/pallas_call | solution.py:109
  9.8 2.0 %collective-permute-start.1 = (bf16[256,512]{1,0:T(8,128)(2,1)S(1)}, bf16[256,512]{1,0:T(8,128)(2,1)S(1)}, u32[]{:S(2)}, u32[]{:S(2)}) collective-permute-start(bf16[256,512]{1,0:T(8,128)(2,1)S(1)} %get-tuple-element.47), channel_id=1, source_target_pairs={{0,8},{4,12},{8,0},{12,4},{16,24},{20,28},{24,16},{28,20},{1,9},{5... | collective-permute-start | bytes 786440 | tf_op jit(solution)/shard_map/ppermute | solution.py:237
  11.8 6.1 %collective-permute-done.10.refs_5_ = bf16[256,512]{1,0:T(8,128)(2,1)S(1)} collective-permute-done((bf16[256,512]{1,0:T(8,128)(2,1)S(1)}, bf16[256,512]{1,0:T(8,128)(2,1)S(1)}, u32[]{:S(2)}, u32[]{:S(2)}) %collective-permute-start.10) | collective-permute-done | bytes 262176 | tf_op jit(solution)/shard_map/ppermute | solution.py:237
  17.8 1.7 %collective-permute-start.3 = (bf16[256,512]{1,0:T(8,128)(2,1)S(1)}, bf16[256,512]{1,0:T(8,128)(2,1)S(1)}, u32[]{:S(2)}, u32[]{:S(2)}) collective-permute-start(bf16[256,512]{1,0:T(8,128)(2,1)S(1)} %get-tuple-element.48), channel_id=1, source_target_pairs={{0,16},{4,20},{8,24},{12,28},{16,0},{20,4},{24,8},{28,12},{1,17},{... | collective-permute-start | bytes 786440 | tf_op jit(solution)/shard_map/ppermute | solution.py:237
  19.6 1.4 %collective-permute-start.5 = (bf16[256,512]{1,0:T(8,128)(2,1)S(1)}, bf16[256,512]{1,0:T(8,128)(2,1)S(1)}, u32[]{:S(2)}, u32[]{:S(2)}) collective-permute-start(bf16[256,512]{1,0:T(8,128)(2,1)S(1)} %get-tuple-element.49), channel_id=1, source_target_pairs={{0,24},{4,28},{8,16},{12,20},{16,8},{20,12},{24,0},{28,4},{1,25},{... | collective-permute-start | bytes 786440 | tf_op jit(solution)/shard_map/ppermute | solution.py:237
  21.5 4.3 %collective-permute-done.1.refs_3_ = bf16[256,512]{1,0:T(8,128)(2,1)S(1)} collective-permute-done((bf16[256,512]{1,0:T(8,128)(2,1)S(1)}, bf16[256,512]{1,0:T(8,128)(2,1)S(1)}, u32[]{:S(2)}, u32[]{:S(2)}) %collective-permute-start.1) | collective-permute-done | bytes 262176 | tf_op jit(solution)/shard_map/ppermute | solution.py:237
  25.8 4.2 %collective-permute-done.3.refs_5_ = bf16[256,512]{1,0:T(8,128)(2,1)S(1)} collective-permute-done((bf16[256,512]{1,0:T(8,128)(2,1)S(1)}, bf16[256,512]{1,0:T(8,128)(2,1)S(1)}, u32[]{:S(2)}, u32[]{:S(2)}) %collective-permute-start.3) | collective-permute-done | bytes 262176 | tf_op jit(solution)/shard_map/ppermute | solution.py:237
  30.0 1.5 %collective-permute-done.5.refs_7_ = bf16[256,512]{1,0:T(8,128)(2,1)S(1)} collective-permute-done((bf16[256,512]{1,0:T(8,128)(2,1)S(1)}, bf16[256,512]{1,0:T(8,128)(2,1)S(1)}, u32[]{:S(2)}, u32[]{:S(2)}) %collective-permute-start.5) | collective-permute-done | bytes 262176 | tf_op jit(solution)/shard_map/ppermute | solution.py:237
  32.1 2.3 %collective-permute-start.28 = (bf16[128,512]{1,0:T(8,128)(2,1)S(1)}, bf16[128,512]{1,0:T(8,128)(2,1)S(1)}, u32[]{:S(2)}, u32[]{:S(2)}) collective-permute-start(bf16[128,512]{1,0:T(8,128)(2,1)S(1)} %get-tuple-element.73), channel_id=1, source_target_pairs={{0,4},{4,8},{8,12},{12,16},{16,20},{20,24},{24,28},{1,5},{5,9},{9,... | collective-permute-start | bytes 393224 | tf_op jit(solution)/shard_map/ppermute | solution.py:391
  34.4 1.6 %owner.2 = (bf16[256,512]{1,0:T(8,128)(2,1)S(1)}, bf16[256,512]{1,0:T(8,128)(2,1)S(1)}, bf16[256,512]{1,0:T(8,128)(2,1)S(1)}, bf16[256,512]{1,0:T(8,128)(2,1)S(1)}, f32[2,8,128]{2,1,0:T(8,128)}) custom-call(s32[1,1]{1,0:T(1,128)} %bitcast.refs_0_, bf16[256,512]{1,0:T(8,128)(2,1)S(1)} %get-tuple-element.50.refs_1_, ...), custom_call_target="tpu_custom_call" | custom-call | tf_op jit(solution)/shard_map/owner/pallas_call | solution.py:182
  37.3 4.5 %collective-permute-start.22 = (bf16[256,512]{1,0:T(8,128)(2,1)S(1)}, bf16[256,512]{1,0:T(8,128)(2,1)S(1)}, u32[]{:S(2)}, u32[]{:S(2)}) collective-permute-start(bf16[256,512]{1,0:T(8,128)(2,1)S(1)} %get-tuple-element.61), channel_id=1, source_target_pairs={{0,8},{4,12},{8,0},{12,4},{16,24},{20,28},{24,16},{28,20},{1,9},{5... | collective-permute-start | bytes 786440 | tf_op jit(solution)/shard_map/ppermute | solution.py:237
  44.2 1.9 %owner.3 = (bf16[256,512]{1,0:T(8,128)(2,1)S(1)}, bf16[256,512]{1,0:T(8,128)(2,1)}, bf16[256,512]{1,0:T(8,128)(2,1)}, bf16[256,512]{1,0:T(8,128)(2,1)}, f32[2,8,128]{2,1,0:T(8,128)}) custom-call(s32[1,1]{1,0:T(1,128)} %bitcast.refs_0_, bf16[256,512]{1,0:T(8,128)(2,1)S(1)} %get-tuple-element.46.refs_1_, ...), custom_call_target="tpu_custom_call", output_to_operand_aliasing={{4}: (9, {})} | custom-call | tf_op jit(solution)/shard_map/owner/pallas_call | solution.py:182
  46.1 2.3 %collective-permute-start.15 = (bf16[256,512]{1,0:T(8,128)(2,1)}, bf16[256,512]{1,0:T(8,128)(2,1)S(1)}, u32[]{:S(2)}, u32[]{:S(2)}) collective-permute-start(bf16[256,512]{1,0:T(8,128)(2,1)} %get-tuple-element.56), channel_id=1, source_target_pairs={{0,8},{4,12},{8,0},{12,4},{16,24},{20,28},{24,16},{28,20},{1,9},{5... | collective-permute-start | bytes 786440 | tf_op jit(solution)/shard_map/ppermute | solution.py:237
  48.4 6.1 %collective-permute-done.22.refs_4_ = bf16[256,512]{1,0:T(8,128)(2,1)S(1)} collective-permute-done((bf16[256,512]{1,0:T(8,128)(2,1)S(1)}, bf16[256,512]{1,0:T(8,128)(2,1)S(1)}, u32[]{:S(2)}, u32[]{:S(2)}) %collective-permute-start.22) | collective-permute-done | bytes 262176 | tf_op jit(solution)/shard_map/ppermute | solution.py:237
  54.8 4.2 %collective-permute-start.19 = (bf16[256,512]{1,0:T(8,128)(2,1)}, bf16[256,512]{1,0:T(8,128)(2,1)S(1)}, u32[]{:S(2)}, u32[]{:S(2)}) collective-permute-start(bf16[256,512]{1,0:T(8,128)(2,1)} %get-tuple-element.58), channel_id=1, source_target_pairs={{0,24},{4,28},{8,16},{12,20},{16,8},{20,12},{24,0},{28,4},{1,25},{... | collective-permute-start | bytes 786440 | tf_op jit(solution)/shard_map/ppermute | solution.py:237
  61.0 4.6 %local.1 = (bf16[512,256]{1,0:T(8,128)(2,1)}, bf16[512,256]{1,0:T(8,128)(2,1)}, bf16[512,256]{1,0:T(8,128)(2,1)}, bf16[512,256]{1,0:T(8,128)(2,1)}, f32[32,8,128]{2,1,0:T(8,128)}) custom-call(s32[1,1]{1,0:T(1,128)} %bitcast.1.first_ref, f32[1,128]{1,0:T(1,128)S(1)} %bitcast.3, bf16[512,256]{1,0:T(8,128)(2,1)} %q_ref.1, bf16[512,256]{1,0:T(8,128)(2,1)} %k_ref.1, ...), custom_call_target="tpu_custom_call" | custom-call | tf_op jit(solution)/shard_map/local/pallas_call | solution.py:341
  65.6 5.8 %all-to-all-start = ((f32[32,8,128]{2,1,0:T(8,128)}), f32[32,8,128]{2,1,0:T(8,128)}, u32[]{:S(2)}, u32[]{:S(2)}) async-start(f32[32,8,128]{2,1,0:T(8,128)} %get-tuple-element.79), calls=%async_computation | async-start | bytes 262144 | tf_op jit(solution)/shard_map/all_to_all | solution.py:405
  72.7 7.1 %all-to-all-done = f32[32,8,128]{2,1,0:T(8,128)} async-done(((f32[32,8,128]{2,1,0:T(8,128)}), f32[32,8,128]{2,1,0:T(8,128)}, u32[]{:S(2)}, u32[]{:S(2)}) %all-to-all-start) | async-done | bytes 131104 | tf_op jit(solution)/shard_map/all_to_all | solution.py:405
  79.7 1.5 %slice_reduce_fusion = f32[128]{0:T(128)} fusion(f32[32,8,128]{2,1,0:T(8,128)} %all-to-all-done), kind=kLoop, calls=%fused_computation | loop fusion | flops 3968 | bytes 16896 | tf_op jit(solution)/shard_map/reduce_sum | solution.py:406
  81.2 1.6 %unpack.2 = (bf16[512,256]{1,0:T(8,128)(2,1)}, bf16[512,256]{1,0:T(8,128)(2,1)}, bf16[512,256]{1,0:T(8,128)(2,1)}, bf16[512,256]{1,0:T(8,128)(2,1)}) custom-call(s32[1,1]{1,0:T(1,128)} %bitcast.refs_0_, f32[8,512]{1,0:T(8,128)S(1)} %copy-done.1, bf16[256,512]{1,0:T(8,128)(2,1)S(1)} %get-tuple-element.60.refs_2_, ...), custom_call_target="tpu_custom_call" | custom-call | tf_op jit(solution)/shard_map/unpack/pallas_call | solution.py:223
  82.8 2.7 %unpack.3 = (bf16[512,256]{1,0:T(8,128)(2,1)}, bf16[512,256]{1,0:T(8,128)(2,1)}, bf16[512,256]{1,0:T(8,128)(2,1)}, bf16[512,256]{1,0:T(8,128)(2,1)}) custom-call(s32[1,1]{1,0:T(1,128)} %bitcast.refs_0_, f32[8,512]{1,0:T(8,128)S(1)} %get-tuple-element.45.refs_1_, ...), custom_call_target="tpu_custom_call", output_to_operand_aliasing={{0}: (10, {}), {1}: (11, {}), {2}: (12, {}), {3}: (13, {})} | custom-call | tf_op jit(solution)/shard_map/unpack/pallas_call | solution.py:223
  (52 shorter events, 8.5 us)
Async XLA Ops:
  2.9 15.0 %collective-permute-start.10 = (bf16[256,512]{1,0:T(8,128)(2,1)S(1)}, bf16[256,512]{1,0:T(8,128)(2,1)S(1)}, u32[]{:S(2)}, u32[]{:S(2)}) collective-permute-start(bf16[256,512]{1,0:T(8,128)(2,1)S(1)} %get-tuple-element.52), channel_id=1, source_target_pairs={{0,16},{4,20},{8,24},{12,28},{16,0},{20,4},{24,8},{28,12},{1,17},{... | collective-permute-start | bytes 786440 | tf_op jit(solution)/shard_map/ppermute | solution.py:237
  5.9 13.7 %collective-permute-start.12 = (bf16[256,512]{1,0:T(8,128)(2,1)S(1)}, bf16[256,512]{1,0:T(8,128)(2,1)S(1)}, u32[]{:S(2)}, u32[]{:S(2)}) collective-permute-start(bf16[256,512]{1,0:T(8,128)(2,1)S(1)} %get-tuple-element.53), channel_id=1, source_target_pairs={{0,24},{4,28},{8,16},{12,20},{16,8},{20,12},{24,0},{28,4},{1,25},{... | collective-permute-start | bytes 786440 | tf_op jit(solution)/shard_map/ppermute | solution.py:237
  7.3 13.7 %collective-permute-start.8 = (bf16[256,512]{1,0:T(8,128)(2,1)S(1)}, bf16[256,512]{1,0:T(8,128)(2,1)S(1)}, u32[]{:S(2)}, u32[]{:S(2)}) collective-permute-start(bf16[256,512]{1,0:T(8,128)(2,1)S(1)} %get-tuple-element.51), channel_id=1, source_target_pairs={{0,8},{4,12},{8,0},{12,4},{16,24},{20,28},{24,16},{28,20},{1,9},{5... | collective-permute-start | bytes 786440 | tf_op jit(solution)/shard_map/ppermute | solution.py:237
  7.5 13.6 %collective-permute-start.7 = (bf16[256,512]{1,0:T(8,128)(2,1)S(1)}, bf16[256,512]{1,0:T(8,128)(2,1)S(1)}, u32[]{:S(2)}, u32[]{:S(2)}) collective-permute-start(bf16[256,512]{1,0:T(8,128)(2,1)S(1)} %get-tuple-element.50.refs_1_), channel_id=1, source_target_pairs={{0,4},{4,0},{8,12},{12,8},{16,20},{20,16},{24,28},{28,24},{1,5},{5... | collective-permute-start | bytes 786440 | tf_op jit(solution)/shard_map/ppermute | solution.py:237
  9.8 16.1 %collective-permute-start.1 = (bf16[256,512]{1,0:T(8,128)(2,1)S(1)}, bf16[256,512]{1,0:T(8,128)(2,1)S(1)}, u32[]{:S(2)}, u32[]{:S(2)}) collective-permute-start(bf16[256,512]{1,0:T(8,128)(2,1)S(1)} %get-tuple-element.47), channel_id=1, source_target_pairs={{0,8},{4,12},{8,0},{12,4},{16,24},{20,28},{24,16},{28,20},{1,9},{5... | collective-permute-start | bytes 786440 | tf_op jit(solution)/shard_map/ppermute | solution.py:237
  17.8 12.2 %collective-permute-start.3 = (bf16[256,512]{1,0:T(8,128)(2,1)S(1)}, bf16[256,512]{1,0:T(8,128)(2,1)S(1)}, u32[]{:S(2)}, u32[]{:S(2)}) collective-permute-start(bf16[256,512]{1,0:T(8,128)(2,1)S(1)} %get-tuple-element.48), channel_id=1, source_target_pairs={{0,16},{4,20},{8,24},{12,28},{16,0},{20,4},{24,8},{28,12},{1,17},{... | collective-permute-start | bytes 786440 | tf_op jit(solution)/shard_map/ppermute | solution.py:237
  19.6 11.9 %collective-permute-start.5 = (bf16[256,512]{1,0:T(8,128)(2,1)S(1)}, bf16[256,512]{1,0:T(8,128)(2,1)S(1)}, u32[]{:S(2)}, u32[]{:S(2)}) collective-permute-start(bf16[256,512]{1,0:T(8,128)(2,1)S(1)} %get-tuple-element.49), channel_id=1, source_target_pairs={{0,24},{4,28},{8,16},{12,20},{16,8},{20,12},{24,0},{28,4},{1,25},{... | collective-permute-start | bytes 786440 | tf_op jit(solution)/shard_map/ppermute | solution.py:237
  21.0 10.5 %collective-permute-start.11 = (bf16[256,512]{1,0:T(8,128)(2,1)S(1)}, bf16[256,512]{1,0:T(8,128)(2,1)S(1)}, u32[]{:S(2)}, u32[]{:S(2)}) collective-permute-start(bf16[256,512]{1,0:T(8,128)(2,1)S(1)} %collective-permute-done.10.refs_5_), channel_id=1, source_target_pairs={{0,4},{4,0},{8,12},{12,8},{16,20},{20,16},{24,28},{28,24},{1,5},{5... | collective-permute-start | bytes 786440 | tf_op jit(solution)/shard_map/ppermute | solution.py:237
  21.0 11.0 %collective-permute-start.13 = (bf16[256,512]{1,0:T(8,128)(2,1)S(1)}, bf16[256,512]{1,0:T(8,128)(2,1)S(1)}, u32[]{:S(2)}, u32[]{:S(2)}) collective-permute-start(bf16[256,512]{1,0:T(8,128)(2,1)S(1)} %collective-permute-done.12.refs_7_), channel_id=1, source_target_pairs={{0,4},{4,0},{8,12},{12,8},{16,20},{20,16},{24,28},{28,24},{1,5},{5... | collective-permute-start | bytes 786440 | tf_op jit(solution)/shard_map/ppermute | solution.py:237
  31.5 11.7 %collective-permute-start.4 = (bf16[256,512]{1,0:T(8,128)(2,1)S(1)}, bf16[256,512]{1,0:T(8,128)(2,1)S(1)}, u32[]{:S(2)}, u32[]{:S(2)}) collective-permute-start(bf16[256,512]{1,0:T(8,128)(2,1)S(1)} %collective-permute-done.3.refs_5_), channel_id=1, source_target_pairs={{0,4},{4,0},{8,12},{12,8},{16,20},{20,16},{24,28},{28,24},{1,5},{5... | collective-permute-start | bytes 786440 | tf_op jit(solution)/shard_map/ppermute | solution.py:237
  32.0 12.2 %collective-permute-start.6 = (bf16[256,512]{1,0:T(8,128)(2,1)S(1)}, bf16[256,512]{1,0:T(8,128)(2,1)S(1)}, u32[]{:S(2)}, u32[]{:S(2)}) collective-permute-start(bf16[256,512]{1,0:T(8,128)(2,1)S(1)} %collective-permute-done.5.refs_7_), channel_id=1, source_target_pairs={{0,4},{4,0},{8,12},{12,8},{16,20},{20,16},{24,28},{28,24},{1,5},{5... | collective-permute-start | bytes 786440 | tf_op jit(solution)/shard_map/ppermute | solution.py:237
  37.3 17.2 %collective-permute-start.22 = (bf16[256,512]{1,0:T(8,128)(2,1)S(1)}, bf16[256,512]{1,0:T(8,128)(2,1)S(1)}, u32[]{:S(2)}, u32[]{:S(2)}) collective-permute-start(bf16[256,512]{1,0:T(8,128)(2,1)S(1)} %get-tuple-element.61), channel_id=1, source_target_pairs={{0,8},{4,12},{8,0},{12,4},{16,24},{20,28},{24,16},{28,20},{1,9},{5... | collective-permute-start | bytes 786440 | tf_op jit(solution)/shard_map/ppermute | solution.py:237
  41.8 12.9 %collective-permute-start.24 = (bf16[256,512]{1,0:T(8,128)(2,1)S(1)}, bf16[256,512]{1,0:T(8,128)(2,1)S(1)}, u32[]{:S(2)}, u32[]{:S(2)}) collective-permute-start(bf16[256,512]{1,0:T(8,128)(2,1)S(1)} %get-tuple-element.62), channel_id=1, source_target_pairs={{0,16},{4,20},{8,24},{12,28},{16,0},{20,4},{24,8},{28,12},{1,17},{... | collective-permute-start | bytes 786440 | tf_op jit(solution)/shard_map/ppermute | solution.py:237
  43.2 16.7 %collective-permute-start.26 = (bf16[256,512]{1,0:T(8,128)(2,1)S(1)}, bf16[256,512]{1,0:T(8,128)(2,1)S(1)}, u32[]{:S(2)}, u32[]{:S(2)}) collective-permute-start(bf16[256,512]{1,0:T(8,128)(2,1)S(1)} %get-tuple-element.63), channel_id=1, source_target_pairs={{0,24},{4,28},{8,16},{12,20},{16,8},{20,12},{24,0},{28,4},{1,25},{... | collective-permute-start | bytes 786440 | tf_op jit(solution)/shard_map/ppermute | solution.py:237
  44.2 15.7 %collective-permute-start.21 = (bf16[256,512]{1,0:T(8,128)(2,1)S(1)}, bf16[256,512]{1,0:T(8,128)(2,1)S(1)}, u32[]{:S(2)}, u32[]{:S(2)}) collective-permute-start(bf16[256,512]{1,0:T(8,128)(2,1)S(1)} %get-tuple-element.60.refs_2_), channel_id=1, source_target_pairs={{0,4},{4,0},{8,12},{12,8},{16,20},{20,16},{24,28},{28,24},{1,5},{5... | collective-permute-start | bytes 786440 | tf_op jit(solution)/shard_map/ppermute | solution.py:237
  46.1 25.3 %collective-permute-start.15 = (bf16[256,512]{1,0:T(8,128)(2,1)}, bf16[256,512]{1,0:T(8,128)(2,1)S(1)}, u32[]{:S(2)}, u32[]{:S(2)}) collective-permute-start(bf16[256,512]{1,0:T(8,128)(2,1)} %get-tuple-element.56), channel_id=1, source_target_pairs={{0,8},{4,12},{8,0},{12,4},{16,24},{20,28},{24,16},{28,20},{1,9},{5... | collective-permute-start | bytes 786440 | tf_op jit(solution)/shard_map/ppermute | solution.py:237
  54.5 17.1 %collective-permute-start.17 = (bf16[256,512]{1,0:T(8,128)(2,1)}, bf16[256,512]{1,0:T(8,128)(2,1)S(1)}, u32[]{:S(2)}, u32[]{:S(2)}) collective-permute-start(bf16[256,512]{1,0:T(8,128)(2,1)} %get-tuple-element.57), channel_id=1, source_target_pairs={{0,16},{4,20},{8,24},{12,28},{16,0},{20,4},{24,8},{28,12},{1,17},{... | collective-permute-start | bytes 786440 | tf_op jit(solution)/shard_map/ppermute | solution.py:237
  54.8 17.2 %collective-permute-start.19 = (bf16[256,512]{1,0:T(8,128)(2,1)}, bf16[256,512]{1,0:T(8,128)(2,1)S(1)}, u32[]{:S(2)}, u32[]{:S(2)}) collective-permute-start(bf16[256,512]{1,0:T(8,128)(2,1)} %get-tuple-element.58), channel_id=1, source_target_pairs={{0,24},{4,28},{8,16},{12,20},{16,8},{20,12},{24,0},{28,4},{1,25},{... | collective-permute-start | bytes 786440 | tf_op jit(solution)/shard_map/ppermute | solution.py:237
  59.8 12.3 %collective-permute-start.23 = (bf16[256,512]{1,0:T(8,128)(2,1)S(1)}, bf16[256,512]{1,0:T(8,128)(2,1)S(1)}, u32[]{:S(2)}, u32[]{:S(2)}) collective-permute-start(bf16[256,512]{1,0:T(8,128)(2,1)S(1)} %collective-permute-done.22.refs_4_), channel_id=1, source_target_pairs={{0,4},{4,0},{8,12},{12,8},{16,20},{20,16},{24,28},{28,24},{1,5},{5... | collective-permute-start | bytes 786440 | tf_op jit(solution)/shard_map/ppermute | solution.py:237
  59.9 12.7 %collective-permute-start.25 = (bf16[256,512]{1,0:T(8,128)(2,1)S(1)}, bf16[256,512]{1,0:T(8,128)(2,1)S(1)}, u32[]{:S(2)}, u32[]{:S(2)}) collective-permute-start(bf16[256,512]{1,0:T(8,128)(2,1)S(1)} %collective-permute-done.24.refs_6_), channel_id=1, source_target_pairs={{0,4},{4,0},{8,12},{12,8},{16,20},{20,16},{24,28},{28,24},{1,5},{5... | collective-permute-start | bytes 786440 | tf_op jit(solution)/shard_map/ppermute | solution.py:237
  65.6 14.2 %all-to-all-start = ((f32[32,8,128]{2,1,0:T(8,128)}), f32[32,8,128]{2,1,0:T(8,128)}, u32[]{:S(2)}, u32[]{:S(2)}) async-start(f32[32,8,128]{2,1,0:T(8,128)} %get-tuple-element.79), calls=%async_computation | async-start | bytes 262144 | tf_op jit(solution)/shard_map/all_to_all | solution.py:405
  71.4 11.4 %collective-permute-start.14 = (bf16[256,512]{1,0:T(8,128)(2,1)S(1)}, bf16[256,512]{1,0:T(8,128)(2,1)S(1)}, u32[]{:S(2)}, u32[]{:S(2)}) collective-permute-start(bf16[256,512]{1,0:T(8,128)(2,1)S(1)} %get-tuple-element.55.refs_2_), channel_id=1, source_target_pairs={{0,4},{4,0},{8,12},{12,8},{16,20},{20,16},{24,28},{28,24},{1,5},{5... | collective-permute-start | bytes 786440 | tf_op jit(solution)/shard_map/ppermute | solution.py:237
  72.0 10.8 %collective-permute-start.16 = (bf16[256,512]{1,0:T(8,128)(2,1)S(1)}, bf16[256,512]{1,0:T(8,128)(2,1)}, u32[]{:S(2)}, u32[]{:S(2)}) collective-permute-start(bf16[256,512]{1,0:T(8,128)(2,1)S(1)} %collective-permute-done.15.refs_4_), channel_id=1, source_target_pairs={{0,4},{4,0},{8,12},{12,8},{16,20},{20,16},{24,28},{28,24},{1,5},{5... | collective-permute-start | bytes 786440 | tf_op jit(solution)/shard_map/ppermute | solution.py:237
  72.2 10.6 %collective-permute-start.18 = (bf16[256,512]{1,0:T(8,128)(2,1)S(1)}, bf16[256,512]{1,0:T(8,128)(2,1)}, u32[]{:S(2)}, u32[]{:S(2)}) collective-permute-start(bf16[256,512]{1,0:T(8,128)(2,1)S(1)} %collective-permute-done.17.refs_6_), channel_id=1, source_target_pairs={{0,4},{4,0},{8,12},{12,8},{16,20},{20,16},{24,28},{28,24},{1,5},{5... | collective-permute-start | bytes 786440 | tf_op jit(solution)/shard_map/ppermute | solution.py:237
  (10 other events, 75.1 us)

commit v2 on v1

--- a/solution.py
+++ b/solution.py
@@ -46,11 +46,9 @@
 def pack_kernel(me_ref, ids_ref, slots_ref, q_ref, k_ref, v_ref, g_ref, *refs, head, per_source, halo):
     halo_refs, (flat_ref, *out_refs) = refs[:halo], refs[halo:]
     if halo:
-        *out_refs, lead_ref, tail_ref = out_refs
-        split = (lead_ref, halo_refs[:4]), (tail_ref, halo_refs[4:])
-        for to_ref, from_refs in split:
-            for n, ref in enumerate(from_refs):
-                to_ref[:, n * ref.shape[1] : (n + 1) * ref.shape[1]] = ref[...]
+        *out_refs, tail_ref = out_refs
+        for n, ref in enumerate(halo_refs):
+            tail_ref[:, n * ref.shape[1] : (n + 1) * ref.shape[1]] = ref[...]
     ids = ids_ref[head : head + 1, :]
     tokens = ids.shape[1]
     clusters = slots_ref.shape[1]
@@ -101,11 +99,9 @@
     operands, specs = [], []
     if own:
         columns = own[0].shape[1]
-        first = pl.BlockSpec((WINDOW, columns), lambda i: (0, 0))
-        last = pl.BlockSpec((WINDOW, columns), lambda i: (tokens // WINDOW - 1, 0))
-        operands = [*own, own[1], own[2]]
-        specs = [first] * 4 + [last] * 2
-        shapes += [jax.ShapeDtypeStruct((WINDOW, n * columns), BF16) for n in (4, 2)]
+        operands = [*own]
+        specs = [pl.BlockSpec((WINDOW, columns), lambda i: (tokens // WINDOW - 1, 0))] * len(own)
+        shapes += [jax.ShapeDtypeStruct((WINDOW, len(own) * columns), BF16)]
     flat, *chunks = pl.pallas_call(
         lambda *refs: pack_kernel(*refs, head=head, per_source=per_source, halo=len(operands)),
         grid=(1,),
@@ -268,14 +264,12 @@
     g_ref,
     pk_ref,
     pv_ref,
-    nq_ref,
-    nk_ref,
-    nv_ref,
-    ng_ref,
     out_ref,
     dq_ref,
     dk_ref,
     dv_ref,
+    edge_ref,
+    rest_ref,
     part_ref,
 ):
     tokens, dim = q_ref.shape
@@ -286,18 +280,18 @@
     bias = shift_rows(jnp.broadcast_to(bias_ref[...], size), 1)
     bias_first = jnp.where(early & (first_ref[0, 0] > 0), NEG, bias)
     spots = [slice(b * WINDOW, (b + 1) * WINDOW) for b in range(count)]
-    queries = [q_ref[s] for s in spots] + [nq_ref[...]]
-    cots = [g_ref[s] for s in spots] + [ng_ref[...]]
-    keys = [pk_ref[...]] + [k_ref[s] for s in spots] + [nk_ref[...]]
-    values = [pv_ref[...]] + [v_ref[s] for s in spots] + [nv_ref[...]]
+    queries = [q_ref[s] for s in spots]
+    cots = [g_ref[s] for s in spots]
+    keys = [pk_ref[...]] + [k_ref[s] for s in spots]
+    values = [pv_ref[...]] + [v_ref[s] for s in spots]
     scores = [
         jnp.where(early, dot_nt(keys[b], queries[b]), dot_nt(keys[b + 1], queries[b])) * scaling
         + (bias if b else bias_first)
-        for b in range(count + 1)
+        for b in range(count)
     ]
     dprobs = [
         jnp.where(early, dot_nt(values[b], cots[b]), dot_nt(values[b + 1], cots[b]))
-        for b in range(count + 1)
+        for b in range(count)
     ]
     both = [softmax_down(s, d) for s, d in zip(scores, dprobs)]
     total = both[0][1]
@@ -312,11 +306,18 @@
     ]
     for b, s in enumerate(spots):
         out_ref[s] = (dot_tn(probs[b][0], values[b]) + dot_tn(probs[b][1], values[b + 1])).astype(BF16)
-        dv_ref[s] = (dot_nn(probs[b][1], cots[b]) + dot_nn(probs[b + 1][0], cots[b + 1])).astype(BF16)
-        dk = dot_nn(dscores[b][1], queries[b]) + dot_nn(dscores[b + 1][0], queries[b + 1])
-        dk_ref[s] = (dk * scaling).astype(BF16)
         dq = dot_tn(dscores[b][0], keys[b]) + dot_tn(dscores[b][1], keys[b + 1])
         dq_ref[s] = (dq * scaling).astype(BF16)
+        dk = dot_nn(dscores[b][1], queries[b])
+        dv = dot_nn(probs[b][1], cots[b])
+        if b + 1 < count:
+            dk_ref[s] = ((dk + dot_nn(dscores[b + 1][0], queries[b + 1])) * scaling).astype(BF16)
+            dv_ref[s] = (dv + dot_nn(probs[b + 1][0], cots[b + 1])).astype(BF16)
+        else:
+            rest_ref[:, :dim] = dk * scaling
+            rest_ref[:, dim:] = dv
+    edge_ref[:, :dim] = (dot_nn(dscores[0][0], queries[0]) * scaling).astype(BF16)
+    edge_ref[:, dim:] = dot_nn(probs[0][0], cots[0]).astype(BF16)
     part = jnp.sum(shift_rows(total, -1), axis=0, keepdims=True)
     part = jnp.broadcast_to(part[None], part_ref.shape)
 
@@ -329,10 +330,11 @@
         part_ref[...] += part
 
 
-def local(first, rel_bias, own, behind, ahead, copies):
+def local(first, rel_bias, own, behind, copies):
     tokens, columns = own[0].shape
     heads = columns // HEAD_DIM
     column = pl.BlockSpec((tokens, HEAD_DIM), lambda h: (0, h))
+    both = pl.BlockSpec((WINDOW, 2 * HEAD_DIM), lambda h: (0, h))
 
     def halo(n):
         return pl.BlockSpec((WINDOW, HEAD_DIM), lambda h: (0, n * heads + h))
@@ -341,14 +343,42 @@
     return pl.pallas_call(
         local_kernel,
         grid=(heads,),
-        in_specs=[scalar_spec(), whole(rel_bias)]
-        + [column] * 4
-        + [halo(0), halo(1), halo(0), halo(1), halo(2), halo(3)],
-        out_specs=[column] * 4 + [whole(part)],
-        out_shape=[jax.ShapeDtypeStruct((tokens, columns), BF16)] * 4 + [part],
+        in_specs=[scalar_spec(), whole(rel_bias)] + [column] * 4 + [halo(0), halo(1)],
+        out_specs=[column] * 4 + [both, both, whole(part)],
+        out_shape=[jax.ShapeDtypeStruct((tokens, columns), BF16)] * 4
+        + [jax.ShapeDtypeStruct((WINDOW, 2 * columns), kind) for kind in (BF16, F32)]
+        + [part],
         name="local",
         compiler_params=PARAMS,
-    )(first, rel_bias, *own, behind, behind, ahead, ahead, ahead, ahead)
+    )(first, rel_bias, *own, behind, behind)
+
+
+def finish_kernel(edge_ref, rest_ref, parts_ref, *refs):
+    dk_ref, dv_ref, bias_ref = refs[-3:]
+    total = rest_ref[...] + edge_ref[...].astype(F32)
+    for head in range(dk_ref.shape[1] // HEAD_DIM):
+        to = slice(head * HEAD_DIM, (head + 1) * HEAD_DIM)
+        at = 2 * head * HEAD_DIM
+        dk_ref[:, to] = total[:, at : at + HEAD_DIM].astype(BF16)
+        dv_ref[:, to] = total[:, at + HEAD_DIM : at + 2 * HEAD_DIM].astype(BF16)
+    bias_ref[...] = jnp.sum(parts_ref[...], axis=0)[:1]
+
+
+def finish(edge, rest, parts, grads):
+    tokens, columns = grads[0].shape
+    any_spec = pl.BlockSpec(memory_space=pl.ANY)
+    bias = jax.ShapeDtypeStruct((1, WINDOW), F32)
+    return pl.pallas_call(
+        finish_kernel,
+        grid=(1,),
+        in_specs=[whole(edge), whole(rest), whole(parts)] + [any_spec] * 2,
+        out_specs=[pl.BlockSpec((WINDOW, columns), lambda i: (tokens // WINDOW - 1, 0))] * 2
+        + [whole(bias)],
+        out_shape=[jax.ShapeDtypeStruct(g.shape, g.dtype) for g in grads] + [bias],
+        input_output_aliases={3: 0, 4: 1},
+        name="finish",
+        compiler_params=PARAMS,
+    )(edge, rest, parts, *grads)
 
 
 def shards(
@@ -378,18 +408,15 @@
 
     flats, got = [], []
     for head in range(heads):
-        ends = own if head == heads - 1 else ()
-        flat, chunks = pack(
-            me, clusters, cluster_slot, routed, head, ctx_size, per_source, ends
-        )
+        ends = own[1:3] if head == heads - 1 else ()
+        flat, chunks = pack(me, clusters, cluster_slot, routed, head, ctx_size, per_source, ends)
         flats.append(flat)
         if ends:
-            *chunks, lead, tail = chunks
+            *chunks, tail = chunks
         got.append(send_far(chunks))
     got = [send_near(pairs) for pairs in got]
 
     behind = lax.ppermute(tail, "ctx", [(i, i + 1) for i in range(ctx_size - 1)])
-    ahead = lax.ppermute(lead, "ctx", [(i + 1, i) for i in range(ctx_size - 1)])
 
     centroids, home = (), []
     for head in range(heads):
@@ -399,11 +426,12 @@
     (centroids,) = centroids
 
     first = (lax.axis_index("ctx") == 0).astype(jnp.int32).reshape(1, 1)
-    local_out, local_dq, local_dk, local_dv, part = local(
-        first, rel_bias.reshape(1, WINDOW), own, behind, ahead, device_count
+    local_out, local_dq, *local_grads, edge, rest, part = local(
+        first, rel_bias.reshape(1, WINDOW), own, behind, device_count
     )
+    edge = lax.ppermute(edge, "ctx", [(i + 1, i) for i in range(ctx_size - 1)])
     parts = lax.all_to_all(part, ("ctx", "head"), 0, 0, tiled=True)
-    bias_grad = jnp.sum(parts[:, 0], axis=0)
+    local_dk, local_dv, bias_grad = finish(edge, rest, parts, local_grads)
 
     columns = ()
     for head in range(heads):
@@ -419,7 +447,7 @@
         local_dq,
         local_dk,
         local_dv,
-        bias_grad,
+        bias_grad[0],
     )
 
 

time: 85.8 us -> 87.2 us (1.016)
  blocking collectives: 0 us -> 14 us
  waiting for transfers between devices: 30.1 us -> 24.2 us
  starting transfers between devices: 35.7 us -> 31.2 us
  other arithmetic: 1.46 us -> 0 us
    all_to_all x0 -> x1, blocking collectives: none -> 14 us  [shards(): parts = lax.all_to_all(part, ('ctx', 'head'), 0, 0, tiled=True)]
    all_to_all x1 -> x0, waiting for transfers between devices: 7.05 us -> none  [shards(): parts = lax.all_to_all(part, ('ctx', 'head'), 0, 0, tiled=True)]
    all_to_all x1 -> x0, starting transfers between devices: 5.8 us -> none  [shards(): parts = lax.all_to_all(part, ('ctx', 'head'), 0, 0, tiled=True)]
    reduce_sum x1 -> x0, other arithmetic: 1.46 us -> none  [shards(): bias_grad = jnp.sum(parts[:, 0], axis=0)]
    ppermute x28, starting transfers between devices: 26.2 us -> 27.6 us  [swap(): return lax.ppermute(array, 'ctx', [(i, i ^ mask) for i in range(size)])]
    pallas_call x2, Pallas kernels: 4.23 us -> 3.11 us  [unpack(): pl.pallas_call(lambda *refs: unpack_kernel(*refs, chunks=len(home)), grid...]
  transfers between devices with their start and end apart: 31 -> 30, of which waited for: 7 -> 8; matrix products, arithmetic and copies ran while one was open for 2% -> 0% of each run, Pallas kernels for 14% -> 14%
where the time goes in v2:
time: 87.2 us; the launch traced here: 86.9 us
  starting transfers between devices  31.2 us (36%)
  waiting for transfers between devices  24.2 us (28%)
  Pallas kernels  16.1 us (18%)
  blocking collectives  14 us (16%)
    ppermute x28, starting transfers between devices, swap(): return lax.ppermute(array, 'ctx', [(i, i ^ mask) for i in range(size)])  27.6 us
    ppermute x28, waiting for transfers between devices, swap(): return lax.ppermute(array, 'ctx', [(i, i ^ mask) for i in range(size)])  23.8 us
    all_to_all x1, blocking collectives, shards(): parts = lax.all_to_all(part, ('ctx', 'head'), 0, 0, tiled=True)  14 us
    pallas_call x1, Pallas kernels, local(): pl.pallas_call(local_kernel, grid=(heads,), in_specs=[scalar_spec(), whol...  4.46 us
    pallas_call x2, Pallas kernels, pack(): pl.pallas_call(lambda *refs: pack_kernel(*refs, head=head, per_source=per...  4.4 us
    pallas_call x2, Pallas kernels, owner(): pl.pallas_call(lambda *refs: owner_kernel(*refs, per_source=per_source, s...  3.41 us
    pallas_call x2, Pallas kernels, unpack(): pl.pallas_call(lambda *refs: unpack_kernel(*refs, chunks=len(home)), grid...  3.11 us
    ppermute x1, starting transfers between devices, shards(): lax.ppermute(tail, 'ctx', [(i, i + 1) for i in range(ctx_size - 1)])  2.34 us
  transfers between devices with their start and end apart: 30, of which 8 were waited for; matrix products, arithmetic and copies ran while one was open for 0% of the time, Pallas kernels for 14%

profile of v2, /device:TPU:0, one launch (start us, length us, event | category | flops | bytes accessed | tf_op | source)
XLA Modules:
  0.0 86.9 jit_solution(8503113055068818184)
XLA Ops:
  0.6 2.2 %pack.3 = (f32[8,512]{1,0:T(8,128)S(1)}, bf16[256,512]{1,0:T(8,128)(2,1)S(1)}, bf16[256,512]{1,0:T(8,128)(2,1)S(1)}, bf16[256,512]{1,0:T(8,128)(2,1)S(1)}, bf16[256,512]{1,0:T(8,128)(2,1)S(1)}) custom-call(s32[1,1]{1,0:T(1,128)} %bitcast.refs_0_, s32[2,512]{1,0:T(2,128)} %refs_1_.3, s32[2,64]{1,0:T(2,128)} %refs_2_.3, bf16[512,256]{1,0:T(8,128)(2,1)} %refs_3_.3, ...), custom_call_target="tpu_custom_call" | custom-call | tf_op jit(solution)/shard_map/pack/pallas_call | solution.py:105
  2.9 3.1 %collective-permute-start.10 = (bf16[256,512]{1,0:T(8,128)(2,1)S(1)}, bf16[256,512]{1,0:T(8,128)(2,1)S(1)}, u32[]{:S(2)}, u32[]{:S(2)}) collective-permute-start(bf16[256,512]{1,0:T(8,128)(2,1)S(1)} %get-tuple-element.56), channel_id=1, source_target_pairs={{0,16},{4,20},{8,24},{12,28},{16,0},{20,4},{24,8},{28,12},{1,17},{... | collective-permute-start | bytes 786440 | tf_op jit(solution)/shard_map/ppermute | solution.py:233
  5.9 1.4 %collective-permute-start.12 = (bf16[256,512]{1,0:T(8,128)(2,1)S(1)}, bf16[256,512]{1,0:T(8,128)(2,1)S(1)}, u32[]{:S(2)}, u32[]{:S(2)}) collective-permute-start(bf16[256,512]{1,0:T(8,128)(2,1)S(1)} %get-tuple-element.57), channel_id=1, source_target_pairs={{0,24},{4,28},{8,16},{12,20},{16,8},{20,12},{24,0},{28,4},{1,25},{... | collective-permute-start | bytes 786440 | tf_op jit(solution)/shard_map/ppermute | solution.py:233
  7.5 2.2 %pack.2 = (f32[8,512]{1,0:T(8,128)S(1)}, bf16[256,512]{1,0:T(8,128)(2,1)S(1)}, bf16[256,512]{1,0:T(8,128)(2,1)S(1)}, bf16[256,512]{1,0:T(8,128)(2,1)S(1)}, bf16[...) custom-call(s32[1,1]{1,0:T(1,128)} %bitcast.refs_0_, s32[2,512]{1,0:T(2,128)} %refs_1_.3, s32[2,64]{1,0:T(2,128)} %refs_2_.3, ...), custom_call_target="tpu_custom_call" | custom-call | tf_op jit(solution)/shard_map/pack/pallas_call | solution.py:105
  9.7 2.0 %collective-permute-start.1 = (bf16[256,512]{1,0:T(8,128)(2,1)S(1)}, bf16[256,512]{1,0:T(8,128)(2,1)S(1)}, u32[]{:S(2)}, u32[]{:S(2)}) collective-permute-start(bf16[256,512]{1,0:T(8,128)(2,1)S(1)} %get-tuple-element.51), channel_id=1, source_target_pairs={{0,8},{4,12},{8,0},{12,4},{16,24},{20,28},{24,16},{28,20},{1,9},{5... | collective-permute-start | bytes 786440 | tf_op jit(solution)/shard_map/ppermute | solution.py:233
  11.7 6.2 %collective-permute-done.10.refs_5_ = bf16[256,512]{1,0:T(8,128)(2,1)S(1)} collective-permute-done((bf16[256,512]{1,0:T(8,128)(2,1)S(1)}, bf16[256,512]{1,0:T(8,128)(2,1)S(1)}, u32[]{:S(2)}, u32[]{:S(2)}) %collective-permute-start.10) | collective-permute-done | bytes 262176 | tf_op jit(solution)/shard_map/ppermute | solution.py:233
  17.8 1.7 %collective-permute-start.3 = (bf16[256,512]{1,0:T(8,128)(2,1)S(1)}, bf16[256,512]{1,0:T(8,128)(2,1)S(1)}, u32[]{:S(2)}, u32[]{:S(2)}) collective-permute-start(bf16[256,512]{1,0:T(8,128)(2,1)S(1)} %get-tuple-element.52), channel_id=1, source_target_pairs={{0,16},{4,20},{8,24},{12,28},{16,0},{20,4},{24,8},{28,12},{1,17},{... | collective-permute-start | bytes 786440 | tf_op jit(solution)/shard_map/ppermute | solution.py:233
  19.6 1.4 %collective-permute-start.5 = (bf16[256,512]{1,0:T(8,128)(2,1)S(1)}, bf16[256,512]{1,0:T(8,128)(2,1)S(1)}, u32[]{:S(2)}, u32[]{:S(2)}) collective-permute-start(bf16[256,512]{1,0:T(8,128)(2,1)S(1)} %get-tuple-element.53), channel_id=1, source_target_pairs={{0,24},{4,28},{8,16},{12,20},{16,8},{20,12},{24,0},{28,4},{1,25},{... | collective-permute-start | bytes 786440 | tf_op jit(solution)/shard_map/ppermute | solution.py:233
  21.5 4.3 %collective-permute-done.1.refs_3_ = bf16[256,512]{1,0:T(8,128)(2,1)S(1)} collective-permute-done((bf16[256,512]{1,0:T(8,128)(2,1)S(1)}, bf16[256,512]{1,0:T(8,128)(2,1)S(1)}, u32[]{:S(2)}, u32[]{:S(2)}) %collective-permute-start.1) | collective-permute-done | bytes 262176 | tf_op jit(solution)/shard_map/ppermute | solution.py:233
  25.8 4.2 %collective-permute-done.3.refs_5_ = bf16[256,512]{1,0:T(8,128)(2,1)S(1)} collective-permute-done((bf16[256,512]{1,0:T(8,128)(2,1)S(1)}, bf16[256,512]{1,0:T(8,128)(2,1)S(1)}, u32[]{:S(2)}, u32[]{:S(2)}) %collective-permute-start.3) | collective-permute-done | bytes 262176 | tf_op jit(solution)/shard_map/ppermute | solution.py:233
  30.0 1.5 %collective-permute-done.5.refs_7_ = bf16[256,512]{1,0:T(8,128)(2,1)S(1)} collective-permute-done((bf16[256,512]{1,0:T(8,128)(2,1)S(1)}, bf16[256,512]{1,0:T(8,128)(2,1)S(1)}, u32[]{:S(2)}, u32[]{:S(2)}) %collective-permute-start.5) | collective-permute-done | bytes 262176 | tf_op jit(solution)/shard_map/ppermute | solution.py:233
  32.1 2.3 %collective-permute-start.28 = (bf16[128,512]{1,0:T(8,128)(2,1)S(1)}, bf16[128,512]{1,0:T(8,128)(2,1)S(1)}, u32[]{:S(2)}, u32[]{:S(2)}) collective-permute-start(bf16[128,512]{1,0:T(8,128)(2,1)S(1)} %get-tuple-element.77), channel_id=1, source_target_pairs={{0,4},{4,8},{8,12},{12,16},{16,20},{20,24},{24,28},{1,5},{5,9},{9,... | collective-permute-start | bytes 393224 | tf_op jit(solution)/shard_map/ppermute | solution.py:419
  34.4 1.9 %owner.2 = (bf16[256,512]{1,0:T(8,128)(2,1)S(1)}, bf16[256,512]{1,0:T(8,128)(2,1)}, bf16[256,512]{1,0:T(8,128)(2,1)}, bf16[256,512]{1,0:T(8,128)(2,1)}, f32[2,8,128]{2,1,0:T(8,128)}) custom-call(s32[1,1]{1,0:T(1,128)} %bitcast.refs_0_, bf16[256,512]{1,0:T(8,128)(2,1)S(1)} %get-tuple-element.54.refs_1_, bf16[256,512]{1,0:T(8,128)(2,1)S(1)} %collective-permute-done.7.refs_2_, ...), custom_call_target="tpu_custom_call" | custom-call | tf_op jit(solution)/shard_map/owner/pallas_call | solution.py:178
  36.3 3.5 %collective-permute-start.22 = (bf16[256,512]{1,0:T(8,128)(2,1)}, bf16[256,512]{1,0:T(8,128)(2,1)S(1)}, u32[]{:S(2)}, u32[]{:S(2)}) collective-permute-start(bf16[256,512]{1,0:T(8,128)(2,1)} %get-tuple-element.65), channel_id=1, source_target_pairs={{0,8},{4,12},{8,0},{12,4},{16,24},{20,28},{24,16},{28,20},{1,9},{5... | collective-permute-start | bytes 786440 | tf_op jit(solution)/shard_map/ppermute | solution.py:233
  42.9 4.5 %local.1 = (bf16[512,256]{1,0:T(8,128)(2,1)}, bf16[512,256]{1,0:T(8,128)(2,1)}, bf16[512,256]{1,0:T(8,128)(2,1)}, bf16[512,256]{1,0:T(8,128)(2,1)}, bf16[128,512...) custom-call(s32[1,1]{1,0:T(1,128)} %bitcast.1.first_ref, f32[1,128]{1,0:T(1,128)S(1)} %bitcast.4, ...), custom_call_target="tpu_custom_call" | custom-call | tf_op jit(solution)/shard_map/local/pallas_call | solution.py:343
  48.6 1.5 %owner.3 = (bf16[256,512]{1,0:T(8,128)(2,1)S(1)}, bf16[256,512]{1,0:T(8,128)(2,1)S(1)}, bf16[256,512]{1,0:T(8,128)(2,1)S(1)}, bf16[256,512]{1,0:T(8,128)(2,1)S(1)}, f32[2,8,128]{2,1,0:T(8,128)}) custom-call(s32[1,1]{1,0:T(1,128)} %bitcast.refs_0_, bf16[256,512]{1,0:T(8,128)(2,1)S(1)} %get-tuple-element.50.refs_1_, ...), custom_call_target="tpu_custom_call", output_to_operand_aliasing={{4}: (9, {})} | custom-call | tf_op jit(solution)/shard_map/owner/pallas_call | solution.py:178
  50.6 3.3 %collective-permute-start.15 = (bf16[256,512]{1,0:T(8,128)(2,1)S(1)}, bf16[256,512]{1,0:T(8,128)(2,1)S(1)}, u32[]{:S(2)}, u32[]{:S(2)}) collective-permute-start(bf16[256,512]{1,0:T(8,128)(2,1)S(1)} %get-tuple-element.60), channel_id=1, source_target_pairs={{0,8},{4,12},{8,0},{12,4},{16,24},{20,28},{24,16},{28,20},{1,9},{5... | collective-permute-start | bytes 786440 | tf_op jit(solution)/shard_map/ppermute | solution.py:233
  53.9 2.0 %collective-permute-start.17 = (bf16[256,512]{1,0:T(8,128)(2,1)S(1)}, bf16[256,512]{1,0:T(8,128)(2,1)S(1)}, u32[]{:S(2)}, u32[]{:S(2)}) collective-permute-start(bf16[256,512]{1,0:T(8,128)(2,1)S(1)} %get-tuple-element.61), channel_id=1, source_target_pairs={{0,16},{4,20},{8,24},{12,28},{16,0},{20,4},{24,8},{28,12},{1,17},{... | collective-permute-start | bytes 786440 | tf_op jit(solution)/shard_map/ppermute | solution.py:233
  57.1 2.3 %collective-permute-done.15.refs_4_ = bf16[256,512]{1,0:T(8,128)(2,1)S(1)} collective-permute-done((bf16[256,512]{1,0:T(8,128)(2,1)S(1)}, bf16[256,512]{1,0:T(8,128)(2,1)S(1)}, u32[]{:S(2)}, u32[]{:S(2)}) %collective-permute-start.15) | collective-permute-done | bytes 262176 | tf_op jit(solution)/shard_map/ppermute | solution.py:233
  59.5 3.3 %collective-permute-start.14 = (bf16[256,512]{1,0:T(8,128)(2,1)S(1)}, bf16[256,512]{1,0:T(8,128)(2,1)S(1)}, u32[]{:S(2)}, u32[]{:S(2)}) collective-permute-start(bf16[256,512]{1,0:T(8,128)(2,1)S(1)} %get-tuple-element.59.refs_2_), channel_id=1, source_target_pairs={{0,4},{4,0},{8,12},{12,8},{16,20},{20,16},{24,28},{28,24},{1,5},{5... | collective-permute-start | bytes 786440 | tf_op jit(solution)/shard_map/ppermute | solution.py:233
  62.7 4.8 %collective-permute-done.17.refs_6_ = bf16[256,512]{1,0:T(8,128)(2,1)S(1)} collective-permute-done((bf16[256,512]{1,0:T(8,128)(2,1)S(1)}, bf16[256,512]{1,0:T(8,128)(2,1)S(1)}, u32[]{:S(2)}, u32[]{:S(2)}) %collective-permute-start.17) | collective-permute-done | bytes 262176 | tf_op jit(solution)/shard_map/ppermute | solution.py:233
  69.0 14.0 %all_to_all.5.parts_ref = f32[32,8,128]{2,1,0:T(8,128)S(1)} all-to-all(f32[32,8,128]{2,1,0:T(8,128)S(1)} %get-tuple-element.82), channel_id=1, replica_groups=mesh['ctx'=8,'head'=4] {'ctx','head'}, dimensions={0} | all-to-all | bytes 262144 | tf_op jit(solution)/shard_map/all_to_all | solution.py:433
  83.7 1.6 %unpack.2 = (bf16[512,256]{1,0:T(8,128)(2,1)}, bf16[512,256]{1,0:T(8,128)(2,1)}, bf16[512,256]{1,0:T(8,128)(2,1)}, bf16[512,256]{1,0:T(8,128)(2,1)}) custom-call(s32[1,1]{1,0:T(1,128)} %bitcast.refs_0_, f32[8,512]{1,0:T(8,128)S(1)} %copy-done.1, bf16[256,512]{1,0:T(8,128)(2,1)S(1)} %get-tuple-element.64.refs_2_, ...), custom_call_target="tpu_custom_call" | custom-call | tf_op jit(solution)/shard_map/unpack/pallas_call | solution.py:219
  85.3 1.6 %unpack.3 = (bf16[512,256]{1,0:T(8,128)(2,1)}, bf16[512,256]{1,0:T(8,128)(2,1)}, bf16[512,256]{1,0:T(8,128)(2,1)}, bf16[512,256]{1,0:T(8,128)(2,1)}) custom-call(s32[1,1]{1,0:T(1,128)} %bitcast.refs_0_, f32[8,512]{1,0:T(8,128)S(1)} %get-tuple-element.49.refs_1_, ...), custom_call_target="tpu_custom_call", output_to_operand_aliasing={{0}: (10, {}), {1}: (11, {}), {2}: (12, {}), {3}: (13, {})} | custom-call | tf_op jit(solution)/shard_map/unpack/pallas_call | solution.py:219
  (51 shorter events, 9.5 us)
Async XLA Ops:
  2.9 15.0 %collective-permute-start.10 = (bf16[256,512]{1,0:T(8,128)(2,1)S(1)}, bf16[256,512]{1,0:T(8,128)(2,1)S(1)}, u32[]{:S(2)}, u32[]{:S(2)}) collective-permute-start(bf16[256,512]{1,0:T(8,128)(2,1)S(1)} %get-tuple-element.56), channel_id=1, source_target_pairs={{0,16},{4,20},{8,24},{12,28},{16,0},{20,4},{24,8},{28,12},{1,17},{... | collective-permute-start | bytes 786440 | tf_op jit(solution)/shard_map/ppermute | solution.py:233
  5.9 13.7 %collective-permute-start.12 = (bf16[256,512]{1,0:T(8,128)(2,1)S(1)}, bf16[256,512]{1,0:T(8,128)(2,1)S(1)}, u32[]{:S(2)}, u32[]{:S(2)}) collective-permute-start(bf16[256,512]{1,0:T(8,128)(2,1)S(1)} %get-tuple-element.57), channel_id=1, source_target_pairs={{0,24},{4,28},{8,16},{12,20},{16,8},{20,12},{24,0},{28,4},{1,25},{... | collective-permute-start | bytes 786440 | tf_op jit(solution)/shard_map/ppermute | solution.py:233
  7.3 13.7 %collective-permute-start.8 = (bf16[256,512]{1,0:T(8,128)(2,1)S(1)}, bf16[256,512]{1,0:T(8,128)(2,1)S(1)}, u32[]{:S(2)}, u32[]{:S(2)}) collective-permute-start(bf16[256,512]{1,0:T(8,128)(2,1)S(1)} %get-tuple-element.55), channel_id=1, source_target_pairs={{0,8},{4,12},{8,0},{12,4},{16,24},{20,28},{24,16},{28,20},{1,9},{5... | collective-permute-start | bytes 786440 | tf_op jit(solution)/shard_map/ppermute | solution.py:233
  7.5 13.6 %collective-permute-start.7 = (bf16[256,512]{1,0:T(8,128)(2,1)S(1)}, bf16[256,512]{1,0:T(8,128)(2,1)S(1)}, u32[]{:S(2)}, u32[]{:S(2)}) collective-permute-start(bf16[256,512]{1,0:T(8,128)(2,1)S(1)} %get-tuple-element.54.refs_1_), channel_id=1, source_target_pairs={{0,4},{4,0},{8,12},{12,8},{16,20},{20,16},{24,28},{28,24},{1,5},{5... | collective-permute-start | bytes 786440 | tf_op jit(solution)/shard_map/ppermute | solution.py:233
  9.7 16.2 %collective-permute-start.1 = (bf16[256,512]{1,0:T(8,128)(2,1)S(1)}, bf16[256,512]{1,0:T(8,128)(2,1)S(1)}, u32[]{:S(2)}, u32[]{:S(2)}) collective-permute-start(bf16[256,512]{1,0:T(8,128)(2,1)S(1)} %get-tuple-element.51), channel_id=1, source_target_pairs={{0,8},{4,12},{8,0},{12,4},{16,24},{20,28},{24,16},{28,20},{1,9},{5... | collective-permute-start | bytes 786440 | tf_op jit(solution)/shard_map/ppermute | solution.py:233
  17.8 12.2 %collective-permute-start.3 = (bf16[256,512]{1,0:T(8,128)(2,1)S(1)}, bf16[256,512]{1,0:T(8,128)(2,1)S(1)}, u32[]{:S(2)}, u32[]{:S(2)}) collective-permute-start(bf16[256,512]{1,0:T(8,128)(2,1)S(1)} %get-tuple-element.52), channel_id=1, source_target_pairs={{0,16},{4,20},{8,24},{12,28},{16,0},{20,4},{24,8},{28,12},{1,17},{... | collective-permute-start | bytes 786440 | tf_op jit(solution)/shard_map/ppermute | solution.py:233
  19.6 11.9 %collective-permute-start.5 = (bf16[256,512]{1,0:T(8,128)(2,1)S(1)}, bf16[256,512]{1,0:T(8,128)(2,1)S(1)}, u32[]{:S(2)}, u32[]{:S(2)}) collective-permute-start(bf16[256,512]{1,0:T(8,128)(2,1)S(1)} %get-tuple-element.53), channel_id=1, source_target_pairs={{0,24},{4,28},{8,16},{12,20},{16,8},{20,12},{24,0},{28,4},{1,25},{... | collective-permute-start | bytes 786440 | tf_op jit(solution)/shard_map/ppermute | solution.py:233
  21.0 10.5 %collective-permute-start.11 = (bf16[256,512]{1,0:T(8,128)(2,1)S(1)}, bf16[256,512]{1,0:T(8,128)(2,1)S(1)}, u32[]{:S(2)}, u32[]{:S(2)}) collective-permute-start(bf16[256,512]{1,0:T(8,128)(2,1)S(1)} %collective-permute-done.10.refs_5_), channel_id=1, source_target_pairs={{0,4},{4,0},{8,12},{12,8},{16,20},{20,16},{24,28},{28,24},{1,5},{5... | collective-permute-start | bytes 786440 | tf_op jit(solution)/shard_map/ppermute | solution.py:233
  21.0 11.0 %collective-permute-start.13 = (bf16[256,512]{1,0:T(8,128)(2,1)S(1)}, bf16[256,512]{1,0:T(8,128)(2,1)S(1)}, u32[]{:S(2)}, u32[]{:S(2)}) collective-permute-start(bf16[256,512]{1,0:T(8,128)(2,1)S(1)} %collective-permute-done.12.refs_7_), channel_id=1, source_target_pairs={{0,4},{4,0},{8,12},{12,8},{16,20},{20,16},{24,28},{28,24},{1,5},{5... | collective-permute-start | bytes 786440 | tf_op jit(solution)/shard_map/ppermute | solution.py:233
  31.5 10.7 %collective-permute-start.4 = (bf16[256,512]{1,0:T(8,128)(2,1)S(1)}, bf16[256,512]{1,0:T(8,128)(2,1)S(1)}, u32[]{:S(2)}, u32[]{:S(2)}) collective-permute-start(bf16[256,512]{1,0:T(8,128)(2,1)S(1)} %collective-permute-done.3.refs_5_), channel_id=1, source_target_pairs={{0,4},{4,0},{8,12},{12,8},{16,20},{20,16},{24,28},{28,24},{1,5},{5... | collective-permute-start | bytes 786440 | tf_op jit(solution)/shard_map/ppermute | solution.py:233
  32.0 15.3 %collective-permute-start.6 = (bf16[256,512]{1,0:T(8,128)(2,1)S(1)}, bf16[256,512]{1,0:T(8,128)(2,1)S(1)}, u32[]{:S(2)}, u32[]{:S(2)}) collective-permute-start(bf16[256,512]{1,0:T(8,128)(2,1)S(1)} %collective-permute-done.5.refs_7_), channel_id=1, source_target_pairs={{0,4},{4,0},{8,12},{12,8},{16,20},{20,16},{24,28},{28,24},{1,5},{5... | collective-permute-start | bytes 786440 | tf_op jit(solution)/shard_map/ppermute | solution.py:233
  36.3 17.6 %collective-permute-start.22 = (bf16[256,512]{1,0:T(8,128)(2,1)}, bf16[256,512]{1,0:T(8,128)(2,1)S(1)}, u32[]{:S(2)}, u32[]{:S(2)}) collective-permute-start(bf16[256,512]{1,0:T(8,128)(2,1)} %get-tuple-element.65), channel_id=1, source_target_pairs={{0,8},{4,12},{8,0},{12,4},{16,24},{20,28},{24,16},{28,20},{1,9},{5... | collective-permute-start | bytes 786440 | tf_op jit(solution)/shard_map/ppermute | solution.py:233
  39.8 16.0 %collective-permute-start.24 = (bf16[256,512]{1,0:T(8,128)(2,1)}, bf16[256,512]{1,0:T(8,128)(2,1)S(1)}, u32[]{:S(2)}, u32[]{:S(2)}) collective-permute-start(bf16[256,512]{1,0:T(8,128)(2,1)} %get-tuple-element.66), channel_id=1, source_target_pairs={{0,16},{4,20},{8,24},{12,28},{16,0},{20,4},{24,8},{28,12},{1,17},{... | collective-permute-start | bytes 786440 | tf_op jit(solution)/shard_map/ppermute | solution.py:233
  41.2 14.8 %collective-permute-start.26 = (bf16[256,512]{1,0:T(8,128)(2,1)}, bf16[256,512]{1,0:T(8,128)(2,1)S(1)}, u32[]{:S(2)}, u32[]{:S(2)}) collective-permute-start(bf16[256,512]{1,0:T(8,128)(2,1)} %get-tuple-element.67), channel_id=1, source_target_pairs={{0,24},{4,28},{8,16},{12,20},{16,8},{20,12},{24,0},{28,4},{1,25},{... | collective-permute-start | bytes 786440 | tf_op jit(solution)/shard_map/ppermute | solution.py:233
  42.2 14.9 %collective-permute-start.21 = (bf16[256,512]{1,0:T(8,128)(2,1)S(1)}, bf16[256,512]{1,0:T(8,128)(2,1)S(1)}, u32[]{:S(2)}, u32[]{:S(2)}) collective-permute-start(bf16[256,512]{1,0:T(8,128)(2,1)S(1)} %get-tuple-element.64.refs_2_), channel_id=1, source_target_pairs={{0,4},{4,0},{8,12},{12,8},{16,20},{20,16},{24,28},{28,24},{1,5},{5... | collective-permute-start | bytes 786440 | tf_op jit(solution)/shard_map/ppermute | solution.py:233
  53.9 13.6 %collective-permute-start.17 = (bf16[256,512]{1,0:T(8,128)(2,1)S(1)}, bf16[256,512]{1,0:T(8,128)(2,1)S(1)}, u32[]{:S(2)}, u32[]{:S(2)}) collective-permute-start(bf16[256,512]{1,0:T(8,128)(2,1)S(1)} %get-tuple-element.61), channel_id=1, source_target_pairs={{0,16},{4,20},{8,24},{12,28},{16,0},{20,4},{24,8},{28,12},{1,17},{... | collective-permute-start | bytes 786440 | tf_op jit(solution)/shard_map/ppermute | solution.py:233
  55.8 12.2 %collective-permute-start.19 = (bf16[256,512]{1,0:T(8,128)(2,1)S(1)}, bf16[256,512]{1,0:T(8,128)(2,1)S(1)}, u32[]{:S(2)}, u32[]{:S(2)}) collective-permute-start(bf16[256,512]{1,0:T(8,128)(2,1)S(1)} %get-tuple-element.62), channel_id=1, source_target_pairs={{0,24},{4,28},{8,16},{12,20},{16,8},{20,12},{24,0},{28,4},{1,25},{... | collective-permute-start | bytes 786440 | tf_op jit(solution)/shard_map/ppermute | solution.py:233
  56.0 12.5 %collective-permute-start.23 = (bf16[256,512]{1,0:T(8,128)(2,1)S(1)}, bf16[256,512]{1,0:T(8,128)(2,1)S(1)}, u32[]{:S(2)}, u32[]{:S(2)}) collective-permute-start(bf16[256,512]{1,0:T(8,128)(2,1)S(1)} %collective-permute-done.22.refs_4_), channel_id=1, source_target_pairs={{0,4},{4,0},{8,12},{12,8},{16,20},{20,16},{24,28},{28,24},{1,5},{5... | collective-permute-start | bytes 786440 | tf_op jit(solution)/shard_map/ppermute | solution.py:233
  57.1 11.5 %collective-permute-start.25 = (bf16[256,512]{1,0:T(8,128)(2,1)S(1)}, bf16[256,512]{1,0:T(8,128)(2,1)S(1)}, u32[]{:S(2)}, u32[]{:S(2)}) collective-permute-start(bf16[256,512]{1,0:T(8,128)(2,1)S(1)} %collective-permute-done.24.refs_6_), channel_id=1, source_target_pairs={{0,4},{4,0},{8,12},{12,8},{16,20},{20,16},{24,28},{28,24},{1,5},{5... | collective-permute-start | bytes 786440 | tf_op jit(solution)/shard_map/ppermute | solution.py:233
  59.5 25.8 %collective-permute-start.14 = (bf16[256,512]{1,0:T(8,128)(2,1)S(1)}, bf16[256,512]{1,0:T(8,128)(2,1)S(1)}, u32[]{:S(2)}, u32[]{:S(2)}) collective-permute-start(bf16[256,512]{1,0:T(8,128)(2,1)S(1)} %get-tuple-element.59.refs_2_), channel_id=1, source_target_pairs={{0,4},{4,0},{8,12},{12,8},{16,20},{20,16},{24,28},{28,24},{1,5},{5... | collective-permute-start | bytes 786440 | tf_op jit(solution)/shard_map/ppermute | solution.py:233
  67.5 16.2 %collective-permute-start.27 = (bf16[256,512]{1,0:T(8,128)(2,1)S(1)}, bf16[256,512]{1,0:T(8,128)(2,1)S(1)}, u32[]{:S(2)}, u32[]{:S(2)}) collective-permute-start(bf16[256,512]{1,0:T(8,128)(2,1)S(1)} %collective-permute-done.26.refs_8_), channel_id=1, source_target_pairs={{0,4},{4,0},{8,12},{12,8},{16,20},{20,16},{24,28},{28,24},{1,5},{5... | collective-permute-start | bytes 786440 | tf_op jit(solution)/shard_map/ppermute | solution.py:233
  68.0 17.3 %collective-permute-start.16 = (bf16[256,512]{1,0:T(8,128)(2,1)S(1)}, bf16[256,512]{1,0:T(8,128)(2,1)S(1)}, u32[]{:S(2)}, u32[]{:S(2)}) collective-permute-start(bf16[256,512]{1,0:T(8,128)(2,1)S(1)} %collective-permute-done.15.refs_4_), channel_id=1, source_target_pairs={{0,4},{4,0},{8,12},{12,8},{16,20},{20,16},{24,28},{28,24},{1,5},{5... | collective-permute-start | bytes 786440 | tf_op jit(solution)/shard_map/ppermute | solution.py:233
  68.5 16.8 %collective-permute-start.18 = (bf16[256,512]{1,0:T(8,128)(2,1)S(1)}, bf16[256,512]{1,0:T(8,128)(2,1)S(1)}, u32[]{:S(2)}, u32[]{:S(2)}) collective-permute-start(bf16[256,512]{1,0:T(8,128)(2,1)S(1)} %collective-permute-done.17.refs_6_), channel_id=1, source_target_pairs={{0,4},{4,0},{8,12},{12,8},{16,20},{20,16},{24,28},{28,24},{1,5},{5... | collective-permute-start | bytes 786440 | tf_op jit(solution)/shard_map/ppermute | solution.py:233
  68.5 16.8 %collective-permute-start.20 = (bf16[256,512]{1,0:T(8,128)(2,1)S(1)}, bf16[256,512]{1,0:T(8,128)(2,1)S(1)}, u32[]{:S(2)}, u32[]{:S(2)}) collective-permute-start(bf16[256,512]{1,0:T(8,128)(2,1)S(1)} %collective-permute-done.19.refs_8_), channel_id=1, source_target_pairs={{0,4},{4,0},{8,12},{12,8},{16,20},{20,16},{24,28},{28,24},{1,5},{5... | collective-permute-start | bytes 786440 | tf_op jit(solution)/shard_map/ppermute | solution.py:233
  (9 other events, 50.4 us)

commit v3 on v2

--- a/solution.py
+++ b/solution.py
@@ -88,6 +88,11 @@
     return pl.BlockSpec(array.shape, lambda *_: (0,) * array.ndim)
 
 
+def halves(arrays):
+    rows, width = arrays[0].shape
+    return [pl.BlockSpec((rows // 2, width), lambda i, m=m: (m % 2, 0)) for m in range(len(arrays))]
+
+
 def pack(me, ids, slots, arrays, head, dests, per_source, own):
     tokens = arrays[0].shape[0]
     clusters = slots.shape[1]
@@ -120,7 +125,7 @@
     centroid_ref = refs[-1]
     dim = HEAD_DIM
     capacity = sources * per_source
-    rows = got_refs[0].shape[0] // 2
+    rows = got_refs[0].shape[0]
     clusters = rows // per_source
     key = iota((capacity, capacity), 0)
     query = iota((capacity, capacity), 1)
@@ -135,8 +140,7 @@
         at = slice(part * dim, (part + 1) * dim)
         return [
             jnp.concatenate(
-                [ref[m % 2 * rows + spot : m % 2 * rows + spot + per_source, at] for m, ref in enumerate(got_refs)],
-                axis=0,
+                [ref[spot : spot + per_source, at] for ref in got_refs], axis=0
             )
             for spot in spots
         ]
@@ -178,7 +182,7 @@
     *back, centroids = pl.pallas_call(
         lambda *refs: owner_kernel(*refs, per_source=per_source, sources=len(got)),
         grid=(1,),
-        in_specs=[scalar_spec()] + [whole(g) for g in got] + [any_spec] * len(previous),
+        in_specs=[scalar_spec()] + halves(got) + [any_spec] * len(previous),
         out_specs=[whole(s) for s in shapes]
         + [pl.BlockSpec((1,) + held.shape[1:], lambda i: (head, 0, 0))],
         out_shape=shapes + [held],
@@ -194,7 +198,7 @@
     width = home_refs[0].shape[1]
     out_refs = refs[-(width // HEAD_DIM) :]
     tokens = flat_ref.shape[1]
-    rows = home_refs[0].shape[0] // 2
+    rows = home_refs[0].shape[0]
     wide = jnp.broadcast_to(flat_ref[:1, :], (HEAD_DIM, tokens)).T.astype(jnp.int32)[:, :rows]
     lane = iota((tokens, rows), 1)
     chosen = jnp.concatenate(
@@ -204,9 +208,7 @@
         ],
         axis=1,
     )
-    home = jnp.concatenate(
-        [ref[m % 2 * rows : (m % 2 + 1) * rows] for m, ref in enumerate(home_refs)], axis=0
-    )
+    home = jnp.concatenate([ref[...] for ref in home_refs], axis=0)
     moved = dot_nn(chosen, home).astype(BF16)
     for n, out_ref in enumerate(out_refs):
         out_ref[...] = moved[:, n * HEAD_DIM : (n + 1) * HEAD_DIM]
@@ -219,7 +221,7 @@
     return pl.pallas_call(
         lambda *refs: unpack_kernel(*refs, chunks=len(home)),
         grid=(1,),
-        in_specs=[scalar_spec(), whole(flat)] + [whole(h) for h in home] + [any_spec] * len(previous),
+        in_specs=[scalar_spec(), whole(flat)] + halves(home) + [any_spec] * len(previous),
         out_specs=[pl.BlockSpec((tokens, HEAD_DIM), lambda i: (0, head))] * outs,
         out_shape=[jax.ShapeDtypeStruct((tokens, heads * HEAD_DIM), BF16)] * outs,
         input_output_aliases={2 + len(home) + n: n for n in range(len(previous))},
@@ -404,7 +406,7 @@
     in_hbm = lambda arrays: tuple(pltpu.with_memory_space_constraint(a, pltpu.HBM) for a in arrays)
     routed = in_hbm((routed_q, routed_k, routed_v, routed_grad))
     own = in_hbm((local_q, local_k, local_v, local_grad))
-    clusters, cluster_slot = in_hbm((clusters, cluster_slot))
+    clusters, cluster_slot, bias_row = in_hbm((clusters, cluster_slot, rel_bias.reshape(1, WINDOW)))
 
     flats, got = [], []
     for head in range(heads):
@@ -427,7 +429,7 @@
 
     first = (lax.axis_index("ctx") == 0).astype(jnp.int32).reshape(1, 1)
     local_out, local_dq, *local_grads, edge, rest, part = local(
-        first, rel_bias.reshape(1, WINDOW), own, behind, device_count
+        first, bias_row, own, behind, device_count
     )
     edge = lax.ppermute(edge, "ctx", [(i + 1, i) for i in range(ctx_size - 1)])
     parts = lax.all_to_all(part, ("ctx", "head"), 0, 0, tiled=True)

time: 87.2 us -> 86.5 us (level)
  no operation moved by 1% of the time
where the time goes in v3:
time: 86.5 us; the launch traced here: 86.2 us
  starting transfers between devices  31.2 us (36%)
  waiting for transfers between devices  24.2 us (28%)
  Pallas kernels  16.1 us (19%)
  blocking collectives  14 us (16%)
    ppermute x28, starting transfers between devices, swap(): return lax.ppermute(array, 'ctx', [(i, i ^ mask) for i in range(size)])  27.6 us
    ppermute x28, waiting for transfers between devices, swap(): return lax.ppermute(array, 'ctx', [(i, i ^ mask) for i in range(size)])  23.8 us
    all_to_all x1, blocking collectives, shards(): parts = lax.all_to_all(part, ('ctx', 'head'), 0, 0, tiled=True)  14 us
    pallas_call x1, Pallas kernels, local(): pl.pallas_call(local_kernel, grid=(heads,), in_specs=[scalar_spec(), whol...  4.47 us
    pallas_call x2, Pallas kernels, pack(): pl.pallas_call(lambda *refs: pack_kernel(*refs, head=head, per_source=per...  4.4 us
    pallas_call x2, Pallas kernels, owner(): pl.pallas_call(lambda *refs: owner_kernel(*refs, per_source=per_source, s...  3.4 us
    pallas_call x2, Pallas kernels, unpack(): pl.pallas_call(lambda *refs: unpack_kernel(*refs, chunks=len(home)), grid...  3.12 us
    ppermute x1, starting transfers between devices, shards(): lax.ppermute(tail, 'ctx', [(i, i + 1) for i in range(ctx_size - 1)])  2.34 us
  transfers between devices with their start and end apart: 30, of which 8 were waited for; matrix products, arithmetic and copies ran while one was open for 0% of the time, Pallas kernels for 14%

profile of v3, /device:TPU:0, one launch (start us, length us, event | category | flops | bytes accessed | tf_op | source)
XLA Modules:
  0.0 86.2 jit_solution(6953659158027348847)
XLA Ops:
  0.6 2.2 %pack.3 = (f32[8,512]{1,0:T(8,128)S(1)}, bf16[256,512]{1,0:T(8,128)(2,1)S(1)}, bf16[256,512]{1,0:T(8,128)(2,1)S(1)}, bf16[256,512]{1,0:T(8,128)(2,1)S(1)}, bf16[256,512]{1,0:T(8,128)(2,1)S(1)}) custom-call(s32[1,1]{1,0:T(1,128)} %bitcast.refs_0_, s32[2,512]{1,0:T(2,128)} %refs_1_.3, s32[2,64]{1,0:T(2,128)} %refs_2_.3, bf16[512,256]{1,0:T(8,128)(2,1)} %refs_3_.3, ...), custom_call_target="tpu_custom_call" | custom-call | tf_op jit(solution)/shard_map/pack/pallas_call | solution.py:110
  2.9 3.1 %collective-permute-start.10 = (bf16[256,512]{1,0:T(8,128)(2,1)S(1)}, bf16[256,512]{1,0:T(8,128)(2,1)S(1)}, u32[]{:S(2)}, u32[]{:S(2)}) collective-permute-start(bf16[256,512]{1,0:T(8,128)(2,1)S(1)} %get-tuple-element.56), channel_id=1, source_target_pairs={{0,16},{4,20},{8,24},{12,28},{16,0},{20,4},{24,8},{28,12},{1,17},{... | collective-permute-start | bytes 786440 | tf_op jit(solution)/shard_map/ppermute | solution.py:235
  5.9 1.4 %collective-permute-start.12 = (bf16[256,512]{1,0:T(8,128)(2,1)S(1)}, bf16[256,512]{1,0:T(8,128)(2,1)S(1)}, u32[]{:S(2)}, u32[]{:S(2)}) collective-permute-start(bf16[256,512]{1,0:T(8,128)(2,1)S(1)} %get-tuple-element.57), channel_id=1, source_target_pairs={{0,24},{4,28},{8,16},{12,20},{16,8},{20,12},{24,0},{28,4},{1,25},{... | collective-permute-start | bytes 786440 | tf_op jit(solution)/shard_map/ppermute | solution.py:235
  7.5 2.2 %pack.2 = (f32[8,512]{1,0:T(8,128)S(1)}, bf16[256,512]{1,0:T(8,128)(2,1)S(1)}, bf16[256,512]{1,0:T(8,128)(2,1)S(1)}, bf16[256,512]{1,0:T(8,128)(2,1)S(1)}, bf16[...) custom-call(s32[1,1]{1,0:T(1,128)} %bitcast.refs_0_, s32[2,512]{1,0:T(2,128)} %refs_1_.3, s32[2,64]{1,0:T(2,128)} %refs_2_.3, ...), custom_call_target="tpu_custom_call" | custom-call | tf_op jit(solution)/shard_map/pack/pallas_call | solution.py:110
  9.7 2.0 %collective-permute-start.1 = (bf16[256,512]{1,0:T(8,128)(2,1)S(1)}, bf16[256,512]{1,0:T(8,128)(2,1)S(1)}, u32[]{:S(2)}, u32[]{:S(2)}) collective-permute-start(bf16[256,512]{1,0:T(8,128)(2,1)S(1)} %get-tuple-element.51), channel_id=1, source_target_pairs={{0,8},{4,12},{8,0},{12,4},{16,24},{20,28},{24,16},{28,20},{1,9},{5... | collective-permute-start | bytes 786440 | tf_op jit(solution)/shard_map/ppermute | solution.py:235
  11.7 6.2 %collective-permute-done.10.refs_5_ = bf16[256,512]{1,0:T(8,128)(2,1)S(1)} collective-permute-done((bf16[256,512]{1,0:T(8,128)(2,1)S(1)}, bf16[256,512]{1,0:T(8,128)(2,1)S(1)}, u32[]{:S(2)}, u32[]{:S(2)}) %collective-permute-start.10) | collective-permute-done | bytes 262176 | tf_op jit(solution)/shard_map/ppermute | solution.py:235
  17.8 1.7 %collective-permute-start.3 = (bf16[256,512]{1,0:T(8,128)(2,1)S(1)}, bf16[256,512]{1,0:T(8,128)(2,1)S(1)}, u32[]{:S(2)}, u32[]{:S(2)}) collective-permute-start(bf16[256,512]{1,0:T(8,128)(2,1)S(1)} %get-tuple-element.52), channel_id=1, source_target_pairs={{0,16},{4,20},{8,24},{12,28},{16,0},{20,4},{24,8},{28,12},{1,17},{... | collective-permute-start | bytes 786440 | tf_op jit(solution)/shard_map/ppermute | solution.py:235
  19.6 1.4 %collective-permute-start.5 = (bf16[256,512]{1,0:T(8,128)(2,1)S(1)}, bf16[256,512]{1,0:T(8,128)(2,1)S(1)}, u32[]{:S(2)}, u32[]{:S(2)}) collective-permute-start(bf16[256,512]{1,0:T(8,128)(2,1)S(1)} %get-tuple-element.53), channel_id=1, source_target_pairs={{0,24},{4,28},{8,16},{12,20},{16,8},{20,12},{24,0},{28,4},{1,25},{... | collective-permute-start | bytes 786440 | tf_op jit(solution)/shard_map/ppermute | solution.py:235
  21.5 4.3 %collective-permute-done.1.refs_3_ = bf16[256,512]{1,0:T(8,128)(2,1)S(1)} collective-permute-done((bf16[256,512]{1,0:T(8,128)(2,1)S(1)}, bf16[256,512]{1,0:T(8,128)(2,1)S(1)}, u32[]{:S(2)}, u32[]{:S(2)}) %collective-permute-start.1) | collective-permute-done | bytes 262176 | tf_op jit(solution)/shard_map/ppermute | solution.py:235
  25.8 4.2 %collective-permute-done.3.refs_5_ = bf16[256,512]{1,0:T(8,128)(2,1)S(1)} collective-permute-done((bf16[256,512]{1,0:T(8,128)(2,1)S(1)}, bf16[256,512]{1,0:T(8,128)(2,1)S(1)}, u32[]{:S(2)}, u32[]{:S(2)}) %collective-permute-start.3) | collective-permute-done | bytes 262176 | tf_op jit(solution)/shard_map/ppermute | solution.py:235
  30.0 1.5 %collective-permute-done.5.refs_7_ = bf16[256,512]{1,0:T(8,128)(2,1)S(1)} collective-permute-done((bf16[256,512]{1,0:T(8,128)(2,1)S(1)}, bf16[256,512]{1,0:T(8,128)(2,1)S(1)}, u32[]{:S(2)}, u32[]{:S(2)}) %collective-permute-start.5) | collective-permute-done | bytes 262176 | tf_op jit(solution)/shard_map/ppermute | solution.py:235
  32.1 2.3 %collective-permute-start.28 = (bf16[128,512]{1,0:T(8,128)(2,1)S(1)}, bf16[128,512]{1,0:T(8,128)(2,1)S(1)}, u32[]{:S(2)}, u32[]{:S(2)}) collective-permute-start(bf16[128,512]{1,0:T(8,128)(2,1)S(1)} %get-tuple-element.77), channel_id=1, source_target_pairs={{0,4},{4,8},{8,12},{12,16},{16,20},{20,24},{24,28},{1,5},{5,9},{9,... | collective-permute-start | bytes 393224 | tf_op jit(solution)/shard_map/ppermute | solution.py:421
  34.4 1.9 %owner.2 = (bf16[256,512]{1,0:T(8,128)(2,1)S(1)}, bf16[256,512]{1,0:T(8,128)(2,1)}, bf16[256,512]{1,0:T(8,128)(2,1)}, bf16[256,512]{1,0:T(8,128)(2,1)}, f32[2,8,128]{2,1,0:T(8,128)}) custom-call(s32[1,1]{1,0:T(1,128)} %bitcast.refs_0_, bf16[256,512]{1,0:T(8,128)(2,1)S(1)} %get-tuple-element.54.refs_1_, bf16[256,512]{1,0:T(8,128)(2,1)S(1)} %collective-permute-done.7.refs_2_, ...), custom_call_target="tpu_custom_call" | custom-call | tf_op jit(solution)/shard_map/owner/pallas_call | solution.py:182
  36.3 3.5 %collective-permute-start.22 = (bf16[256,512]{1,0:T(8,128)(2,1)}, bf16[256,512]{1,0:T(8,128)(2,1)S(1)}, u32[]{:S(2)}, u32[]{:S(2)}) collective-permute-start(bf16[256,512]{1,0:T(8,128)(2,1)} %get-tuple-element.65), channel_id=1, source_target_pairs={{0,8},{4,12},{8,0},{12,4},{16,24},{20,28},{24,16},{28,20},{1,9},{5... | collective-permute-start | bytes 786440 | tf_op jit(solution)/shard_map/ppermute | solution.py:235
  42.2 4.5 %local.1 = (bf16[512,256]{1,0:T(8,128)(2,1)}, bf16[512,256]{1,0:T(8,128)(2,1)}, bf16[512,256]{1,0:T(8,128)(2,1)}, bf16[512,256]{1,0:T(8,128)(2,1)}, bf16[128,512...) custom-call(s32[1,1]{1,0:T(1,128)} %bitcast.1.first_ref, f32[1,128]{1,0:T(1,128)} %bitcast.4, ...), custom_call_target="tpu_custom_call" | custom-call | tf_op jit(solution)/shard_map/local/pallas_call | solution.py:345
  48.0 1.5 %owner.3 = (bf16[256,512]{1,0:T(8,128)(2,1)S(1)}, bf16[256,512]{1,0:T(8,128)(2,1)S(1)}, bf16[256,512]{1,0:T(8,128)(2,1)S(1)}, bf16[256,512]{1,0:T(8,128)(2,1)S(1)}, f32[2,8,128]{2,1,0:T(8,128)}) custom-call(s32[1,1]{1,0:T(1,128)} %bitcast.refs_0_, bf16[256,512]{1,0:T(8,128)(2,1)S(1)} %get-tuple-element.50.refs_1_, ...), custom_call_target="tpu_custom_call", output_to_operand_aliasing={{4}: (9, {})} | custom-call | tf_op jit(solution)/shard_map/owner/pallas_call | solution.py:182
  49.9 3.3 %collective-permute-start.15 = (bf16[256,512]{1,0:T(8,128)(2,1)S(1)}, bf16[256,512]{1,0:T(8,128)(2,1)S(1)}, u32[]{:S(2)}, u32[]{:S(2)}) collective-permute-start(bf16[256,512]{1,0:T(8,128)(2,1)S(1)} %get-tuple-element.60), channel_id=1, source_target_pairs={{0,8},{4,12},{8,0},{12,4},{16,24},{20,28},{24,16},{28,20},{1,9},{5... | collective-permute-start | bytes 786440 | tf_op jit(solution)/shard_map/ppermute | solution.py:235
  53.2 2.0 %collective-permute-start.17 = (bf16[256,512]{1,0:T(8,128)(2,1)S(1)}, bf16[256,512]{1,0:T(8,128)(2,1)S(1)}, u32[]{:S(2)}, u32[]{:S(2)}) collective-permute-start(bf16[256,512]{1,0:T(8,128)(2,1)S(1)} %get-tuple-element.61), channel_id=1, source_target_pairs={{0,16},{4,20},{8,24},{12,28},{16,0},{20,4},{24,8},{28,12},{1,17},{... | collective-permute-start | bytes 786440 | tf_op jit(solution)/shard_map/ppermute | solution.py:235
  56.5 2.3 %collective-permute-done.15.refs_4_ = bf16[256,512]{1,0:T(8,128)(2,1)S(1)} collective-permute-done((bf16[256,512]{1,0:T(8,128)(2,1)S(1)}, bf16[256,512]{1,0:T(8,128)(2,1)S(1)}, u32[]{:S(2)}, u32[]{:S(2)}) %collective-permute-start.15) | collective-permute-done | bytes 262176 | tf_op jit(solution)/shard_map/ppermute | solution.py:235
  58.8 3.3 %collective-permute-start.14 = (bf16[256,512]{1,0:T(8,128)(2,1)S(1)}, bf16[256,512]{1,0:T(8,128)(2,1)S(1)}, u32[]{:S(2)}, u32[]{:S(2)}) collective-permute-start(bf16[256,512]{1,0:T(8,128)(2,1)S(1)} %get-tuple-element.59.refs_2_), channel_id=1, source_target_pairs={{0,4},{4,0},{8,12},{12,8},{16,20},{20,16},{24,28},{28,24},{1,5},{5... | collective-permute-start | bytes 786440 | tf_op jit(solution)/shard_map/ppermute | solution.py:235
  62.1 4.8 %collective-permute-done.17.refs_6_ = bf16[256,512]{1,0:T(8,128)(2,1)S(1)} collective-permute-done((bf16[256,512]{1,0:T(8,128)(2,1)S(1)}, bf16[256,512]{1,0:T(8,128)(2,1)S(1)}, u32[]{:S(2)}, u32[]{:S(2)}) %collective-permute-start.17) | collective-permute-done | bytes 262176 | tf_op jit(solution)/shard_map/ppermute | solution.py:235
  68.4 14.0 %all_to_all.5.parts_ref = f32[32,8,128]{2,1,0:T(8,128)S(1)} all-to-all(f32[32,8,128]{2,1,0:T(8,128)S(1)} %get-tuple-element.82), channel_id=1, replica_groups=mesh['ctx'=8,'head'=4] {'ctx','head'}, dimensions={0} | all-to-all | bytes 262144 | tf_op jit(solution)/shard_map/all_to_all | solution.py:435
  83.1 1.6 %unpack.2 = (bf16[512,256]{1,0:T(8,128)(2,1)}, bf16[512,256]{1,0:T(8,128)(2,1)}, bf16[512,256]{1,0:T(8,128)(2,1)}, bf16[512,256]{1,0:T(8,128)(2,1)}) custom-call(s32[1,1]{1,0:T(1,128)} %bitcast.refs_0_, f32[8,512]{1,0:T(8,128)S(1)} %copy-done.1, bf16[256,512]{1,0:T(8,128)(2,1)S(1)} %get-tuple-element.64.refs_2_, ...), custom_call_target="tpu_custom_call" | custom-call | tf_op jit(solution)/shard_map/unpack/pallas_call | solution.py:221
  84.7 1.6 %unpack.3 = (bf16[512,256]{1,0:T(8,128)(2,1)}, bf16[512,256]{1,0:T(8,128)(2,1)}, bf16[512,256]{1,0:T(8,128)(2,1)}, bf16[512,256]{1,0:T(8,128)(2,1)}) custom-call(s32[1,1]{1,0:T(1,128)} %bitcast.refs_0_, f32[8,512]{1,0:T(8,128)S(1)} %get-tuple-element.49.refs_1_, ...), custom_call_target="tpu_custom_call", output_to_operand_aliasing={{0}: (10, {}), {1}: (11, {}), {2}: (12, {}), {3}: (13, {})} | custom-call | tf_op jit(solution)/shard_map/unpack/pallas_call | solution.py:221
  (49 shorter events, 8.8 us)
Async XLA Ops:
  2.9 15.0 %collective-permute-start.10 = (bf16[256,512]{1,0:T(8,128)(2,1)S(1)}, bf16[256,512]{1,0:T(8,128)(2,1)S(1)}, u32[]{:S(2)}, u32[]{:S(2)}) collective-permute-start(bf16[256,512]{1,0:T(8,128)(2,1)S(1)} %get-tuple-element.56), channel_id=1, source_target_pairs={{0,16},{4,20},{8,24},{12,28},{16,0},{20,4},{24,8},{28,12},{1,17},{... | collective-permute-start | bytes 786440 | tf_op jit(solution)/shard_map/ppermute | solution.py:235
  5.9 13.7 %collective-permute-start.12 = (bf16[256,512]{1,0:T(8,128)(2,1)S(1)}, bf16[256,512]{1,0:T(8,128)(2,1)S(1)}, u32[]{:S(2)}, u32[]{:S(2)}) collective-permute-start(bf16[256,512]{1,0:T(8,128)(2,1)S(1)} %get-tuple-element.57), channel_id=1, source_target_pairs={{0,24},{4,28},{8,16},{12,20},{16,8},{20,12},{24,0},{28,4},{1,25},{... | collective-permute-start | bytes 786440 | tf_op jit(solution)/shard_map/ppermute | solution.py:235
  7.3 13.7 %collective-permute-start.8 = (bf16[256,512]{1,0:T(8,128)(2,1)S(1)}, bf16[256,512]{1,0:T(8,128)(2,1)S(1)}, u32[]{:S(2)}, u32[]{:S(2)}) collective-permute-start(bf16[256,512]{1,0:T(8,128)(2,1)S(1)} %get-tuple-element.55), channel_id=1, source_target_pairs={{0,8},{4,12},{8,0},{12,4},{16,24},{20,28},{24,16},{28,20},{1,9},{5... | collective-permute-start | bytes 786440 | tf_op jit(solution)/shard_map/ppermute | solution.py:235
  7.5 13.6 %collective-permute-start.7 = (bf16[256,512]{1,0:T(8,128)(2,1)S(1)}, bf16[256,512]{1,0:T(8,128)(2,1)S(1)}, u32[]{:S(2)}, u32[]{:S(2)}) collective-permute-start(bf16[256,512]{1,0:T(8,128)(2,1)S(1)} %get-tuple-element.54.refs_1_), channel_id=1, source_target_pairs={{0,4},{4,0},{8,12},{12,8},{16,20},{20,16},{24,28},{28,24},{1,5},{5... | collective-permute-start | bytes 786440 | tf_op jit(solution)/shard_map/ppermute | solution.py:235
  9.7 16.2 %collective-permute-start.1 = (bf16[256,512]{1,0:T(8,128)(2,1)S(1)}, bf16[256,512]{1,0:T(8,128)(2,1)S(1)}, u32[]{:S(2)}, u32[]{:S(2)}) collective-permute-start(bf16[256,512]{1,0:T(8,128)(2,1)S(1)} %get-tuple-element.51), channel_id=1, source_target_pairs={{0,8},{4,12},{8,0},{12,4},{16,24},{20,28},{24,16},{28,20},{1,9},{5... | collective-permute-start | bytes 786440 | tf_op jit(solution)/shard_map/ppermute | solution.py:235
  17.8 12.2 %collective-permute-start.3 = (bf16[256,512]{1,0:T(8,128)(2,1)S(1)}, bf16[256,512]{1,0:T(8,128)(2,1)S(1)}, u32[]{:S(2)}, u32[]{:S(2)}) collective-permute-start(bf16[256,512]{1,0:T(8,128)(2,1)S(1)} %get-tuple-element.52), channel_id=1, source_target_pairs={{0,16},{4,20},{8,24},{12,28},{16,0},{20,4},{24,8},{28,12},{1,17},{... | collective-permute-start | bytes 786440 | tf_op jit(solution)/shard_map/ppermute | solution.py:235
  19.6 11.9 %collective-permute-start.5 = (bf16[256,512]{1,0:T(8,128)(2,1)S(1)}, bf16[256,512]{1,0:T(8,128)(2,1)S(1)}, u32[]{:S(2)}, u32[]{:S(2)}) collective-permute-start(bf16[256,512]{1,0:T(8,128)(2,1)S(1)} %get-tuple-element.53), channel_id=1, source_target_pairs={{0,24},{4,28},{8,16},{12,20},{16,8},{20,12},{24,0},{28,4},{1,25},{... | collective-permute-start | bytes 786440 | tf_op jit(solution)/shard_map/ppermute | solution.py:235
  21.0 10.5 %collective-permute-start.11 = (bf16[256,512]{1,0:T(8,128)(2,1)S(1)}, bf16[256,512]{1,0:T(8,128)(2,1)S(1)}, u32[]{:S(2)}, u32[]{:S(2)}) collective-permute-start(bf16[256,512]{1,0:T(8,128)(2,1)S(1)} %collective-permute-done.10.refs_5_), channel_id=1, source_target_pairs={{0,4},{4,0},{8,12},{12,8},{16,20},{20,16},{24,28},{28,24},{1,5},{5... | collective-permute-start | bytes 786440 | tf_op jit(solution)/shard_map/ppermute | solution.py:235
  21.0 11.0 %collective-permute-start.13 = (bf16[256,512]{1,0:T(8,128)(2,1)S(1)}, bf16[256,512]{1,0:T(8,128)(2,1)S(1)}, u32[]{:S(2)}, u32[]{:S(2)}) collective-permute-start(bf16[256,512]{1,0:T(8,128)(2,1)S(1)} %collective-permute-done.12.refs_7_), channel_id=1, source_target_pairs={{0,4},{4,0},{8,12},{12,8},{16,20},{20,16},{24,28},{28,24},{1,5},{5... | collective-permute-start | bytes 786440 | tf_op jit(solution)/shard_map/ppermute | solution.py:235
  31.5 10.7 %collective-permute-start.4 = (bf16[256,512]{1,0:T(8,128)(2,1)S(1)}, bf16[256,512]{1,0:T(8,128)(2,1)S(1)}, u32[]{:S(2)}, u32[]{:S(2)}) collective-permute-start(bf16[256,512]{1,0:T(8,128)(2,1)S(1)} %collective-permute-done.3.refs_5_), channel_id=1, source_target_pairs={{0,4},{4,0},{8,12},{12,8},{16,20},{20,16},{24,28},{28,24},{1,5},{5... | collective-permute-start | bytes 786440 | tf_op jit(solution)/shard_map/ppermute | solution.py:235
  32.0 14.7 %collective-permute-start.6 = (bf16[256,512]{1,0:T(8,128)(2,1)S(1)}, bf16[256,512]{1,0:T(8,128)(2,1)S(1)}, u32[]{:S(2)}, u32[]{:S(2)}) collective-permute-start(bf16[256,512]{1,0:T(8,128)(2,1)S(1)} %collective-permute-done.5.refs_7_), channel_id=1, source_target_pairs={{0,4},{4,0},{8,12},{12,8},{16,20},{20,16},{24,28},{28,24},{1,5},{5... | collective-permute-start | bytes 786440 | tf_op jit(solution)/shard_map/ppermute | solution.py:235
  36.3 16.9 %collective-permute-start.22 = (bf16[256,512]{1,0:T(8,128)(2,1)}, bf16[256,512]{1,0:T(8,128)(2,1)S(1)}, u32[]{:S(2)}, u32[]{:S(2)}) collective-permute-start(bf16[256,512]{1,0:T(8,128)(2,1)} %get-tuple-element.65), channel_id=1, source_target_pairs={{0,8},{4,12},{8,0},{12,4},{16,24},{20,28},{24,16},{28,20},{1,9},{5... | collective-permute-start | bytes 786440 | tf_op jit(solution)/shard_map/ppermute | solution.py:235
  39.8 15.3 %collective-permute-start.24 = (bf16[256,512]{1,0:T(8,128)(2,1)}, bf16[256,512]{1,0:T(8,128)(2,1)S(1)}, u32[]{:S(2)}, u32[]{:S(2)}) collective-permute-start(bf16[256,512]{1,0:T(8,128)(2,1)} %get-tuple-element.66), channel_id=1, source_target_pairs={{0,16},{4,20},{8,24},{12,28},{16,0},{20,4},{24,8},{28,12},{1,17},{... | collective-permute-start | bytes 786440 | tf_op jit(solution)/shard_map/ppermute | solution.py:235
  41.2 14.1 %collective-permute-start.26 = (bf16[256,512]{1,0:T(8,128)(2,1)}, bf16[256,512]{1,0:T(8,128)(2,1)S(1)}, u32[]{:S(2)}, u32[]{:S(2)}) collective-permute-start(bf16[256,512]{1,0:T(8,128)(2,1)} %get-tuple-element.67), channel_id=1, source_target_pairs={{0,24},{4,28},{8,16},{12,20},{16,8},{20,12},{24,0},{28,4},{1,25},{... | collective-permute-start | bytes 786440 | tf_op jit(solution)/shard_map/ppermute | solution.py:235
  42.2 14.2 %collective-permute-start.21 = (bf16[256,512]{1,0:T(8,128)(2,1)S(1)}, bf16[256,512]{1,0:T(8,128)(2,1)S(1)}, u32[]{:S(2)}, u32[]{:S(2)}) collective-permute-start(bf16[256,512]{1,0:T(8,128)(2,1)S(1)} %get-tuple-element.64.refs_2_), channel_id=1, source_target_pairs={{0,4},{4,0},{8,12},{12,8},{16,20},{20,16},{24,28},{28,24},{1,5},{5... | collective-permute-start | bytes 786440 | tf_op jit(solution)/shard_map/ppermute | solution.py:235
  53.2 13.6 %collective-permute-start.17 = (bf16[256,512]{1,0:T(8,128)(2,1)S(1)}, bf16[256,512]{1,0:T(8,128)(2,1)S(1)}, u32[]{:S(2)}, u32[]{:S(2)}) collective-permute-start(bf16[256,512]{1,0:T(8,128)(2,1)S(1)} %get-tuple-element.61), channel_id=1, source_target_pairs={{0,16},{4,20},{8,24},{12,28},{16,0},{20,4},{24,8},{28,12},{1,17},{... | collective-permute-start | bytes 786440 | tf_op jit(solution)/shard_map/ppermute | solution.py:235
  55.2 12.2 %collective-permute-start.19 = (bf16[256,512]{1,0:T(8,128)(2,1)S(1)}, bf16[256,512]{1,0:T(8,128)(2,1)S(1)}, u32[]{:S(2)}, u32[]{:S(2)}) collective-permute-start(bf16[256,512]{1,0:T(8,128)(2,1)S(1)} %get-tuple-element.62), channel_id=1, source_target_pairs={{0,24},{4,28},{8,16},{12,20},{16,8},{20,12},{24,0},{28,4},{1,25},{... | collective-permute-start | bytes 786440 | tf_op jit(solution)/shard_map/ppermute | solution.py:235
  55.3 12.5 %collective-permute-start.23 = (bf16[256,512]{1,0:T(8,128)(2,1)S(1)}, bf16[256,512]{1,0:T(8,128)(2,1)S(1)}, u32[]{:S(2)}, u32[]{:S(2)}) collective-permute-start(bf16[256,512]{1,0:T(8,128)(2,1)S(1)} %collective-permute-done.22.refs_4_), channel_id=1, source_target_pairs={{0,4},{4,0},{8,12},{12,8},{16,20},{20,16},{24,28},{28,24},{1,5},{5... | collective-permute-start | bytes 786440 | tf_op jit(solution)/shard_map/ppermute | solution.py:235
  56.4 11.5 %collective-permute-start.25 = (bf16[256,512]{1,0:T(8,128)(2,1)S(1)}, bf16[256,512]{1,0:T(8,128)(2,1)S(1)}, u32[]{:S(2)}, u32[]{:S(2)}) collective-permute-start(bf16[256,512]{1,0:T(8,128)(2,1)S(1)} %collective-permute-done.24.refs_6_), channel_id=1, source_target_pairs={{0,4},{4,0},{8,12},{12,8},{16,20},{20,16},{24,28},{28,24},{1,5},{5... | collective-permute-start | bytes 786440 | tf_op jit(solution)/shard_map/ppermute | solution.py:235
  58.8 25.8 %collective-permute-start.14 = (bf16[256,512]{1,0:T(8,128)(2,1)S(1)}, bf16[256,512]{1,0:T(8,128)(2,1)S(1)}, u32[]{:S(2)}, u32[]{:S(2)}) collective-permute-start(bf16[256,512]{1,0:T(8,128)(2,1)S(1)} %get-tuple-element.59.refs_2_), channel_id=1, source_target_pairs={{0,4},{4,0},{8,12},{12,8},{16,20},{20,16},{24,28},{28,24},{1,5},{5... | collective-permute-start | bytes 786440 | tf_op jit(solution)/shard_map/ppermute | solution.py:235
  66.8 16.2 %collective-permute-start.27 = (bf16[256,512]{1,0:T(8,128)(2,1)S(1)}, bf16[256,512]{1,0:T(8,128)(2,1)S(1)}, u32[]{:S(2)}, u32[]{:S(2)}) collective-permute-start(bf16[256,512]{1,0:T(8,128)(2,1)S(1)} %collective-permute-done.26.refs_8_), channel_id=1, source_target_pairs={{0,4},{4,0},{8,12},{12,8},{16,20},{20,16},{24,28},{28,24},{1,5},{5... | collective-permute-start | bytes 786440 | tf_op jit(solution)/shard_map/ppermute | solution.py:235
  67.4 17.3 %collective-permute-start.16 = (bf16[256,512]{1,0:T(8,128)(2,1)S(1)}, bf16[256,512]{1,0:T(8,128)(2,1)S(1)}, u32[]{:S(2)}, u32[]{:S(2)}) collective-permute-start(bf16[256,512]{1,0:T(8,128)(2,1)S(1)} %collective-permute-done.15.refs_4_), channel_id=1, source_target_pairs={{0,4},{4,0},{8,12},{12,8},{16,20},{20,16},{24,28},{28,24},{1,5},{5... | collective-permute-start | bytes 786440 | tf_op jit(solution)/shard_map/ppermute | solution.py:235
  67.8 16.8 %collective-permute-start.18 = (bf16[256,512]{1,0:T(8,128)(2,1)S(1)}, bf16[256,512]{1,0:T(8,128)(2,1)S(1)}, u32[]{:S(2)}, u32[]{:S(2)}) collective-permute-start(bf16[256,512]{1,0:T(8,128)(2,1)S(1)} %collective-permute-done.17.refs_6_), channel_id=1, source_target_pairs={{0,4},{4,0},{8,12},{12,8},{16,20},{20,16},{24,28},{28,24},{1,5},{5... | collective-permute-start | bytes 786440 | tf_op jit(solution)/shard_map/ppermute | solution.py:235
  67.9 16.8 %collective-permute-start.20 = (bf16[256,512]{1,0:T(8,128)(2,1)S(1)}, bf16[256,512]{1,0:T(8,128)(2,1)S(1)}, u32[]{:S(2)}, u32[]{:S(2)}) collective-permute-start(bf16[256,512]{1,0:T(8,128)(2,1)S(1)} %collective-permute-done.19.refs_8_), channel_id=1, source_target_pairs={{0,4},{4,0},{8,12},{12,8},{16,20},{20,16},{24,28},{28,24},{1,5},{5... | collective-permute-start | bytes 786440 | tf_op jit(solution)/shard_map/ppermute | solution.py:235
  (8 other events, 49.7 us)
